TPU v7x, 32 devices: a whole 2x2x4 slice. The times are simulated.
32 devices in a mesh: wide: 8 (over y, x, core), narrow: 4 (over z).
Axes of the slice: x: 2, y: 2, z: 4, core: 2. Of those that a mesh axis runs over, the one named last changes fastest.
Arguments:
- fraction: float32 [3, 32768], P(None, ('wide', 'narrow')), may hold values from 0 to 1
- masses: float32 [32768], P(('wide', 'narrow')), may hold values from 0.05 to 0.5
- leaf_cell: int32 [3, 256], P(None, ('wide', 'narrow')), may hold values from 0 to 255, as said below
- exports: int32 [4, 64], P(None, ('wide', 'narrow')), may hold values from 0 to 8, as said below
- tile_lists: int32 [2, 256], P(None, ('wide', 'narrow')), may hold values from 0 to 7, as said below
Outputs:
- accel: float32 [3, 32768], P(None, ('wide', 'narrow'))
Inputs may be any that keep to these rules, and one draw needn't show every extreme that they name: `leaf_cell`: column n belongs to rank m = n // 8, with wide index m // 4 and narrow index m mod 4: its first entry plus 0 .. 1 lies within that wide index's 32 planes, its second entry plus 0 .. 3 within that narrow index's 64 planes; the third entry is any cell. `exports`: row f and the 2 columns of rank m list distinct local leaf numbers of rank m to be exported across face f, then the value 8 in empty slots; every rank fills all slots of one of its rows. `tile_lists`: column n lists 2 distinct local leaf numbers of rank n // 8.
All inputs are finite; a program needn't handle non-finite values.
Results may differ from a plain program's by a relative error of at most 0.0003.
Values sent between devices are 32-bit elements; how exact they have to be, the bound alone decides.
A program may use at most 64 MiB of HBM per device.

v0:
```python
import math

import jax
import jax.numpy as jnp
from jax import lax
from jax.sharding import PartitionSpec as P

G = 256
PX = 2
PY = 4
PZ = 16


SCREEN = 0.5
SOFTEN = 0.5
PRECISE = lax.Precision.HIGHEST


def from_behind(shard, axis, by):
    peers = lax.axis_size(axis)
    return lax.ppermute(shard, axis, [(i, (i + by) % peers) for i in range(peers)])


def padded_2(cells, sides, width):
    for axis, dim in sides:
        count = lax.axis_size(axis)
        head = lax.slice_in_dim(cells, 0, width, axis=dim)
        tail = lax.slice_in_dim(cells, cells.shape[dim] - width, cells.shape[dim], axis=dim)
        cells = jnp.concatenate(
            [
                lax.ppermute(tail, axis, [(i, (i + 1) % count) for i in range(count)]),
                cells,
                lax.ppermute(head, axis, [((i + 1) % count, i) for i in range(count)]),
            ],
            axis=dim,
        )
    return cells


def tables(length):
    index_row = jnp.arange(length, dtype=jnp.int32)
    phase = index_row[:, None] * index_row[None, :] % length
    phase_angle = phase.astype(jnp.float32) * (2.0 * math.pi / length)
    return (jnp.cos(phase_angle), jnp.sin(phase_angle))


def half_tables(length, depth_count):
    index_row = jnp.arange(length, dtype=jnp.int32)
    index_col = jnp.arange(depth_count, dtype=jnp.int32)
    phase = index_row[:, None] * index_col[None, :] % length
    phase_angle = phase.astype(jnp.float32) * (2.0 * math.pi / length)
    valid = (index_col <= length // 2).astype(jnp.float32)[None, :]
    return (jnp.cos(phase_angle) * valid, jnp.sin(phase_angle) * valid)


def forward(halves, pattern, cosine_table, sine_table):
    real_part, imag_part = halves
    result_real = jnp.einsum(pattern, real_part, cosine_table, precision=PRECISE)
    result_imag = -jnp.einsum(pattern, real_part, sine_table, precision=PRECISE)
    if imag_part is not None:
        result_real = result_real + jnp.einsum(pattern, imag_part, sine_table, precision=PRECISE)
        result_imag = result_imag + jnp.einsum(pattern, imag_part, cosine_table, precision=PRECISE)
    return (result_real, result_imag)


def inverse(halves, pattern, cosine_table, sine_table):
    real_part, imag_part = halves
    result_real = jnp.einsum(pattern, real_part, cosine_table, precision=PRECISE) - jnp.einsum(
        pattern, imag_part, sine_table, precision=PRECISE
    )
    result_imag = jnp.einsum(pattern, imag_part, cosine_table, precision=PRECISE) + jnp.einsum(
        pattern, real_part, sine_table, precision=PRECISE
    )
    return (result_real, result_imag)


def inverse_real(halves, pattern, cosine_table, sine_table):
    real_part, imag_part = halves
    return jnp.einsum(pattern, real_part, cosine_table, precision=PRECISE) - jnp.einsum(
        pattern, imag_part, sine_table, precision=PRECISE
    )


def turn_wide(halves):
    return (
        lax.all_to_all(halves[0], "wide", split_axis=2, concat_axis=3, tiled=True),
        lax.all_to_all(halves[1], "wide", split_axis=2, concat_axis=3, tiled=True),
    )


def turn_narrow(halves):
    return (
        lax.all_to_all(halves[0], "narrow", split_axis=2, concat_axis=3, tiled=True),
        lax.all_to_all(halves[1], "narrow", split_axis=2, concat_axis=3, tiled=True),
    )


def across_wide(payload, offset):
    return from_behind(payload, "wide", offset)


def across_narrow(payload, offset):
    return from_behind(payload, "narrow", offset)


def cic_weights(fraction, extent):
    coordinate = 0.5 + fraction * (extent - 1.0)
    centres = jnp.arange(extent, dtype=jnp.int32).astype(jnp.float32) + 0.5
    return jnp.maximum(0.0, 1.0 - jnp.abs(coordinate[..., None] - centres))


def leaf_positions(cell_table, fraction):
    leaf_total = cell_table.shape[1]
    extents = jnp.asarray([PX - 1.0, PY - 1.0, PZ - 1.0], dtype=jnp.float32)
    scaled = fraction.reshape(3, leaf_total, -1) * extents[:, None, None] + 0.5
    return jnp.transpose(cell_table.astype(jnp.float32)[:, :, None] + scaled, (1, 0, 2))


def tile_block(targets, sources, masses):
    separation = sources[:, :, :, None, :] - targets[:, None, :, :, None]
    separation = separation - G * jnp.floor(separation / G + 0.5)
    squared = jnp.sum(separation * separation, axis=2)
    distance = jnp.sqrt(squared)
    screened = jax.scipy.special.erfc(distance / (2.0 * SCREEN)) + distance / (
        SCREEN * math.sqrt(math.pi)
    ) * jnp.exp(-squared / (4.0 * SCREEN * SCREEN))
    weight = masses[:, :, None, :] * screened / (squared + SOFTEN * SOFTEN) ** 1.5
    return jnp.sum(weight[:, :, None, :, :] * separation, axis=(1, 4))


def tile_forces(targets, sources, masses):
    block_size = 4
    blocks = targets.shape[0] // block_size

    def one_block(blocked):
        return tile_block(blocked[0], blocked[1], blocked[2])

    result = lax.map(
        one_block,
        (
            targets.reshape((blocks, block_size) + targets.shape[1:]),
            sources.reshape((blocks, block_size) + sources.shape[1:]),
            masses.reshape((blocks, block_size) + masses.shape[1:]),
        ),
    )
    return result.reshape(targets.shape)


def green_factor(wave_x, wave_y, wave_z):
    squared_sum = 0.0
    for wavenumber in (wave_x, wave_y, wave_z):
        folded = jnp.where(wavenumber > G // 2, wavenumber - G, wavenumber).astype(jnp.float32) * (
            2.0 * math.pi / G
        )
        squared_sum = squared_sum + folded * folded
    divisor = jnp.where(squared_sum > 0, squared_sum, 1.0)
    return jnp.where(
        squared_sum > 0, -4.0 * math.pi * jnp.exp(-squared_sum * SCREEN * SCREEN) / divisor, 0.0
    )


def local(fraction, masses, leaf_cell, exports, tile_lists):
    leaves = leaf_cell.shape[1]
    members = masses.shape[0] // leaves
    slots = exports.shape[1]
    slab_x = G // lax.axis_size("wide")
    slab_y = G // lax.axis_size("narrow")
    wide_at = lax.axis_index("wide")
    narrow_at = lax.axis_index("narrow")
    positions = leaf_positions(leaf_cell, fraction)
    leaf_mass = masses.reshape(leaves, members)
    own_lists = jnp.transpose(tile_lists)
    chosen = jnp.minimum(exports, leaves - 1)
    filled = (exports < leaves).astype(jnp.float32)
    outgoing = [(positions[chosen[face_index]], chosen[face_index]) for face_index in range(4)]
    arrived = [
        across_wide(outgoing[0], 1),
        across_wide(outgoing[1], -1),
        across_narrow(outgoing[2], 1),
        across_narrow(outgoing[3], -1),
    ]
    short_range = tile_forces(positions, positions[own_lists], leaf_mass[own_lists])
    guests = jnp.concatenate([parcel[0] for parcel in arrived], axis=0)
    guest_ids = jnp.concatenate([parcel[1] for parcel in arrived], axis=0)
    guest_lists = own_lists[guest_ids]
    guest_force = tile_forces(guests, positions[guest_lists], leaf_mass[guest_lists])
    per_face = guest_force.reshape(4, slots, 3, members)
    returned = [
        across_wide(per_face[0], -1),
        across_wide(per_face[1], 1),
        across_narrow(per_face[2], -1),
        across_narrow(per_face[3], 1),
    ]
    for face_index in range(4):
        short_range = short_range.at[chosen[face_index]].add(
            returned[face_index] * filled[face_index][:, None, None]
        )
    local_x = leaf_cell[0] - wide_at * slab_x
    local_y = leaf_cell[1] - narrow_at * slab_y
    cell_x = local_x[:, None] + jnp.arange(PX, dtype=jnp.int32)
    cell_y = local_y[:, None] + jnp.arange(PY, dtype=jnp.int32)
    cell_z = (leaf_cell[2][:, None] + jnp.arange(PZ, dtype=jnp.int32)) % G
    fraction_leaf = fraction.reshape(3, leaves, members)
    weight_x = cic_weights(fraction_leaf[0], PX)
    weight_y = cic_weights(fraction_leaf[1], PY)
    weight_z = cic_weights(fraction_leaf[2], PZ)
    patch_mass = jnp.einsum(
        "np,npa,npb,npc->nabc", leaf_mass, weight_x, weight_y, weight_z, precision=PRECISE
    )
    density = (
        jnp.zeros((slab_x, slab_y, G), jnp.float32)
        .at[cell_x[:, :, None, None], cell_y[:, None, :, None], cell_z[:, None, None, :]]
        .add(patch_mass)
    )
    cosine_table, sine_table = tables(G)
    depth_count = G // 2 + lax.axis_size("narrow")
    depth_cosine, depth_sine = half_tables(G, depth_count)
    depth_index = jnp.arange(depth_count, dtype=jnp.int32)
    mode_weight = jnp.where(
        (depth_index == 0) | (depth_index == G // 2), 1.0, jnp.where(depth_index < G // 2, 2.0, 0.0)
    ).astype(jnp.float32)
    back_cosine = jnp.transpose(depth_cosine) * mode_weight[:, None]
    back_sine = jnp.transpose(depth_sine) * mode_weight[:, None]
    current = forward((density[None], None), "cxyz,zk->cxky", depth_cosine, depth_sine)
    current = turn_narrow(current)
    current = forward(current, "cxzy,yk->czkx", cosine_table, sine_table)
    current = turn_wide(current)
    spectrum = forward(current, "czkx,xj->czkj", cosine_table, sine_table)
    depth_local = spectrum[0].shape[1]
    across = spectrum[0].shape[2]
    wave_z = (narrow_at * depth_local + jnp.arange(depth_local, dtype=jnp.int32))[:, None, None]
    wave_y = (wide_at * across + jnp.arange(across, dtype=jnp.int32))[None, :, None]
    wave_x = jnp.arange(G, dtype=jnp.int32)[None, None, :]
    greens = green_factor(wave_x, wave_y, wave_z)
    potential_real = spectrum[0] * greens
    potential_imag = spectrum[1] * greens
    halves = (potential_real, potential_imag)
    current = inverse(halves, "czkj,jx->czxk", cosine_table, sine_table)
    current = turn_wide(current)
    current = inverse(current, "czxk,ky->cxyz", cosine_table, sine_table)
    current = turn_narrow(current)
    mesh_field = inverse_real(current, "cxyk,kz->cxyz", back_cosine, back_sine)
    mesh_field = mesh_field / float(G * G * G)
    potential = mesh_field[0]
    padded = padded_2(potential, (("wide", 0), ("narrow", 1)), 2)
    centre_y = padded[:, 2 : slab_y + 2]
    accel_x = (
        -(
            8.0 * (centre_y[3 : slab_x + 3] - centre_y[1 : slab_x + 1])
            - (centre_y[4 : slab_x + 4] - centre_y[0:slab_x])
        )
        / 12.0
    )
    centre_x = padded[2 : slab_x + 2]
    accel_y = (
        -(
            8.0 * (centre_x[:, 3 : slab_y + 3] - centre_x[:, 1 : slab_y + 1])
            - (centre_x[:, 4 : slab_y + 4] - centre_x[:, 0:slab_y])
        )
        / 12.0
    )
    accel_z = (
        -(
            8.0 * (jnp.roll(potential, -1, 2) - jnp.roll(potential, 1, 2))
            - (jnp.roll(potential, -2, 2) - jnp.roll(potential, 2, 2))
        )
        / 12.0
    )
    accel_field = jnp.stack([accel_x, accel_y, accel_z])
    sampled = accel_field[
        :, cell_x[:, :, None, None], cell_y[:, None, :, None], cell_z[:, None, None, :]
    ]
    long_range = jnp.einsum(
        "knabc,npa,npb,npc->knp", sampled, weight_x, weight_y, weight_z, precision=PRECISE
    )
    combined = long_range + jnp.transpose(short_range, (1, 0, 2))
    return combined.reshape(3, leaves * members)


def solution(mesh):
    placed = (
        P(None, ("wide", "narrow")),
        P(("wide", "narrow")),
        P(None, ("wide", "narrow")),
        P(None, ("wide", "narrow")),
        P(None, ("wide", "narrow")),
    )
    return jax.shard_map(
        local, mesh=mesh, in_specs=placed, out_specs=P(None, ("wide", "narrow")), check_vma=False
    )
```

profile of v0, /device:TPU:0, one launch (start us, length us, event | category | flops | bytes accessed | tf_op | source)
XLA Modules:
  0.0 520.4 jit_solution(5271777817172542324)
XLA Ops:
  7.9 9.0 %scatter_custom_fusion.4 = f32[524288]{0:T(1024)} fusion(s32[1024]{0:T(1024)S(1)} %reshape.1044, f32[1024]{0:T(1024)S(1)} %reshape.1046, f32[]{:T(128)} %constant.482.clone.1), kind=kCustom, calls=%fused_computation.159 | custom fusion | flops 1024 | bytes 2097156
  22.5 3.7 copy.328
  26.2 4.2 reshape.1088
  30.4 6.4 %all-to-all-start = ((f32[4,1,67584]{2,1,0:T(1,128)}), f32[4,1,67584]{2,1,0:T(1,128)S(1)}, u32[]{:S(2)}, u32[]{:S(2)}) async-start(f32[4,1,67584]{2,1,0:T(1,128)} %reshape.1088), calls=%async_computation | async-start | bytes 2162688 | tf_op jit(solution)/shard_map/all_to_all | solution.py:93
  36.7 3.7 negate_bitcast_fusion
  45.9 17.3 %all-to-all-done = f32[4,1,67584]{2,1,0:T(1,128)S(1)} async-done(((f32[4,1,67584]{2,1,0:T(1,128)}), f32[4,1,67584]{2,1,0:T(1,128)S(1)}, u32[]{:S(2)}, u32[]{:S(2)}) %all-to-all-start) | async-done | bytes 1081376 | tf_op jit(solution)/shard_map/all_to_all | solution.py:93
  63.1 4.3 all-to-all-start.1
  68.2 3.8 collective-permute-start.7
  75.0 3.9 collective-permute-start.11
  79.5 4.6 reduce.26
  93.9 5.6 %reduce.27 = f32[4,67584]{1,0:T(4,128)} reduce(f32[4,1,67584]{2,1,0:T(1,128)} %all-to-all-done.1, f32[]{:T(128)} %broadcast.1504), dimensions={1}, to_apply=%all_to_all.91.reduce_sub_computation | reduce | bytes 2162692 | tf_op jit(solution)/shard_map/all_to_all | solution.py:94
  104.5 11.4 %reshape.1071 = f32[32,33,256]{2,1,0:T(8,128)S(1)} reshape(f32[1,32,33,4,64]{4,3,2,1,0:T(4,128)} %copy.395) | data formatting | bytes 2162688 | tf_op jit(solution)/shard_map/reshape.38
  115.9 4.6 fusion.67
  120.5 5.4 %copy.339 = f32[1,33,256,32]{1,3,0,2:T(8,128)} copy(f32[1,33,256,32]{2,1,3,0:T(8,128)} %fusion.67) | data formatting | bytes 2162688 | tf_op jit(solution)/shard_map/add | solution.py:62
  125.9 6.4 %reshape.1092 = f32[8,1,33792]{2,1,0:T(1,128)} reshape(f32[256,1,32,33]{3,2,1,0:T(8,128)} %bitcast.304) | data formatting | bytes 2162688
  132.3 4.4 all-to-all-start.3
  142.3 4.5 copy.334
  146.8 6.4 %reshape.1094 = f32[8,1,33792]{2,1,0:T(1,128)} reshape(f32[256,1,32,33]{3,2,1,0:T(8,128)} %bitcast.305) | data formatting | bytes 2162688
  153.2 4.5 all-to-all-start.2
  157.9 4.4 reduce.28
  162.2 7.2 %reshape.1093 = f32[256,1,32,33]{3,2,1,0:T(8,128)} reshape(f32[8,33792]{1,0:T(8,128)S(1)} %reduce.28) | data formatting | bytes 2162688
  169.5 6.6 %copy.389 = f32[1,33,8,32,32]{3,2,4,1,0:T(8,128)} copy(f32[1,33,8,32,32]{1,4,3,2,0:T(8,128)} %bitcast.306) | data formatting | bytes 2162688 | tf_op jit(solution)/shard_map/all_to_all | solution.py:87
  176.1 5.9 %copy.341 = f32[1,33,32,8,32]{4,3,2,1,0:T(8,128)} copy(f32[1,33,32,8,32]{2,3,4,1,0:T(8,128)} %bitcast.298) | data formatting | bytes 2162688 | tf_op jit(solution)/shard_map/all_to_all | solution.py:87
  182.0 3.8 reshape.916
  191.9 7.2 %reshape.1095 = f32[256,1,32,33]{3,2,1,0:T(8,128)} reshape(f32[8,33792]{1,0:T(8,128)S(1)} %reduce.29) | data formatting | bytes 2162688
  199.2 6.6 %copy.388 = f32[1,33,8,32,32]{3,2,4,1,0:T(8,128)} copy(f32[1,33,8,32,32]{1,4,3,2,0:T(8,128)} %bitcast.307) | data formatting | bytes 2162688 | tf_op jit(solution)/shard_map/all_to_all | solution.py:86
  205.8 5.9 %copy.336 = f32[1,33,32,8,32]{4,3,2,1,0:T(8,128)} copy(f32[1,33,32,8,32]{2,3,4,1,0:T(8,128)} %bitcast.299) | data formatting | bytes 2162688 | tf_op jit(solution)/shard_map/all_to_all | solution.py:86
  227.1 4.5 copy.350
  231.6 6.4 %reshape.1096 = f32[8,1,33792]{2,1,0:T(1,128)} reshape(f32[256,1,32,33]{3,2,1,0:T(8,128)} %bitcast.308) | data formatting | bytes 2162688
  238.0 4.2 all-to-all-start.5
  242.2 5.7 %while.24 = (s32[]{:T(128)}, f32[2,4,3,128]{3,2,1,0:T(4,128)S(1)}, f32[2,4,2,128]{3,2,1,0:T(2,128)S(1)}, f32[2,4,2,3,128]{4,3,2,1,0:T(4,128)S(1)}, f32[2,4,3,128]{3,1,0,2:T(4,128)S(1)}, /*index=5*/s32[]{:T(128)}) while((s32[]{:T(128)}, f32[2,4,3,128]{3,2,1,0:T(4,128)S(1)}, f32[2,4,2,128]{3,2,1,0:T(2,128)S(1)}, ...), condition=%wide.region_4.5_spmd, body=%wide.region_1.0_spmd.sunk | while | flops 14940674 | bytes 2218077 | solution.py:138
  253.7 4.5 copy.344
  258.2 6.4 %reshape.1098 = f32[8,1,33792]{2,1,0:T(1,128)} reshape(f32[256,1,32,33]{3,2,1,0:T(8,128)} %bitcast.309) | data formatting | bytes 2162688
  264.6 4.7 all-to-all-start.4
  274.5 7.2 %reshape.1097 = f32[256,1,32,33]{3,2,1,0:T(8,128)} reshape(f32[8,33792]{1,0:T(8,128)S(1)} %reduce.30) | data formatting | bytes 2162688
  281.7 6.6 %copy.391 = f32[1,33,8,32,32]{3,2,4,1,0:T(8,128)} copy(f32[1,33,8,32,32]{1,4,3,2,0:T(8,128)} %bitcast.310) | data formatting | bytes 2162688 | tf_op jit(solution)/shard_map/all_to_all | solution.py:87
  288.3 5.9 %copy.399 = f32[1,33,32,8,32]{4,3,1,2,0:T(8,128)} copy(f32[1,33,32,8,32]{2,3,4,1,0:T(8,128)} %bitcast.300) | data formatting | bytes 2162688 | tf_op jit(solution)/shard_map/reshape.64
  294.2 3.8 reshape.1073
  301.4 4.4 reduce.31
  305.7 7.2 %reshape.1099 = f32[256,1,32,33]{3,2,1,0:T(8,128)} reshape(f32[8,33792]{1,0:T(8,128)S(1)} %reduce.31) | data formatting | bytes 2162688
  313.0 6.6 %copy.390 = f32[1,33,8,32,32]{3,2,4,1,0:T(8,128)} copy(f32[1,33,8,32,32]{1,4,3,2,0:T(8,128)} %bitcast.311) | data formatting | bytes 2162688 | tf_op jit(solution)/shard_map/all_to_all | solution.py:86
  319.6 5.9 %copy.398 = f32[1,33,32,8,32]{4,3,1,2,0:T(8,128)} copy(f32[1,33,32,8,32]{2,3,4,1,0:T(8,128)} %bitcast.301) | data formatting | bytes 2162688 | tf_op jit(solution)/shard_map/reshape.58
  325.5 3.9 reshape.1072
  329.3 4.6 fusion.71
  334.0 5.4 %copy.360 = f32[1,32,256,33]{3,1,0,2:T(8,128)} copy(f32[1,32,256,33]{2,3,1,0:T(8,128)} %fusion.71) | data formatting | bytes 2162688 | tf_op jit(solution)/shard_map/add | solution.py:71
  339.4 6.4 %reshape.1100 = f32[4,1,67584]{2,1,0:T(1,128)} reshape(f32[256,1,32,33]{3,2,1,0:T(8,128)} %bitcast.312) | data formatting | bytes 2162688
  345.8 4.4 all-to-all-start.7
  357.2 15.7 %collective-permute-done.10 = f32[2,3,128]{2,1,0:T(4,128)S(1)} collective-permute-done((f32[2,3,128]{2,1,0:T(4,128)S(1)}, f32[2,3,128]{2,1,0:T(4,128)S(1)}, u32[]{:S(2)}, u32[]{:S(2)}) %collective-permute-start.10) | collective-permute-done | bytes 3104 | tf_op jit(solution)/shard_map/ppermute | solution.py:21
  377.9 4.7 copy.354
  382.6 6.4 %reshape.1102 = f32[4,1,67584]{2,1,0:T(1,128)} reshape(f32[256,1,32,33]{3,2,1,0:T(8,128)} %bitcast.313) | data formatting | bytes 2162688
  389.0 6.6 %all-to-all-start.6 = ((f32[4,1,67584]{2,1,0:T(1,128)}), f32[4,1,67584]{2,1,0:T(1,128)}, u32[]{:S(2)}, u32[]{:S(2)}) async-start(f32[4,1,67584]{2,1,0:T(1,128)} %reshape.1102), calls=%async_computation.6 | async-start | bytes 2162688 | tf_op jit(solution)/shard_map/all_to_all | solution.py:93
  395.6 5.7 %while.25 = (s32[]{:T(128)}, f32[2,4,3,128]{3,2,1,0:T(4,128)S(1)}, f32[2,4,2,128]{3,2,1,0:T(2,128)S(1)}, f32[2,4,2,3,128]{4,3,2,1,0:T(4,128)S(1)}, f32[2,4,3,128]{3,2,1,0:T(4,128)S(1)}, /*index=5*/s32[]{:T(128)}) while((s32[]{:T(128)}, f32[2,4,3,128]{3,2,1,0:T(4,128)S(1)}, f32[2,4,2,128]{3,2,1,0:T(2,128)S(1)}, ...), condition=%wide.region_8.9_spmd, body=%wide.region_5.8_spmd.sunk | while | flops 14940674 | bytes 2205789 | solution.py:138
  406.4 6.5 %collective-permute-done.14 = f32[2,3,128]{2,1,0:T(4,128)S(1)} collective-permute-done((f32[2,3,128]{2,1,0:T(4,128)S(1)}, f32[2,3,128]{2,1,0:T(4,128)S(1)}, u32[]{:S(2)}, u32[]{:S(2)}) %collective-permute-start.14) | collective-permute-done | bytes 3104 | tf_op jit(solution)/shard_map/ppermute | solution.py:21
  417.6 4.6 reduce.32
  422.2 7.3 %reshape.1101 = f32[256,1,32,33]{3,2,1,0:T(8,128)} reshape(f32[4,67584]{1,0:T(4,128)S(1)} %reduce.32) | data formatting | bytes 2162688
  429.5 5.3 %copy.393 = f32[1,32,4,64,33]{3,2,1,4,0:T(4,128)} copy(f32[1,32,4,64,33]{4,1,3,2,0:T(8,128)} %bitcast.302) | data formatting | bytes 2162688 | tf_op jit(solution)/shard_map/all_to_all | solution.py:94
  436.7 4.6 reduce.33
  441.4 7.3 %reshape.1103 = f32[256,1,32,33]{3,2,1,0:T(8,128)} reshape(f32[4,67584]{1,0:T(4,128)S(1)} %reduce.33) | data formatting | bytes 2162688
  448.7 5.4 %copy.392 = f32[1,32,4,64,33]{3,2,1,4,0:T(4,128)} copy(f32[1,32,4,64,33]{4,1,3,2,0:T(8,128)} %bitcast.303) | data formatting | bytes 2162688 | tf_op jit(solution)/shard_map/all_to_all | solution.py:93
  456.0 6.4 %fusion.42 = f32[32,64,256]{2,1,0:T(8,128)S(1)} fusion(f32[32,64,132]{1,0,2:T(8,128)S(1)} %bitcast.315, f32[132]{0:T(256)S(1)} %fusion.201, f32[132]{0:T(256)S(1)} %copy-done.13), kind=kOutput, calls=%fused_computation.85 | convolution fusion | flops 831012864 | bytes 3179552 | tf_op jit(solution)/shard_map/cxyk,kz->cxyz/dot_general | solution.py:79
  462.4 6.6 %subtract_multiply_fusion.2 = f32[32,64,256]{2,1,0:T(8,128)S(1)} fusion(f32[32,64,256]{2,1,0:T(8,128)S(1)} %fusion.42, f32[32,64,132]{1,0,2:T(8,128)S(1)} %bitcast.314, f32[132]{0:T(256)S(1)} %fusion.201, f32[132]{0:T(256)S(1)} %copy-done.13), kind=kOutput, calls=%fused_computation.117 | convolution fusion | flops 832061440 | bytes 5276704 | tf_op jit(solution)/shard_map/cxyk,kz->cxyz/dot_general | solution.py:79
  480.6 5.8 %collective-permute-start.3 = (f32[36,2,256]{2,1,0:T(2,128)S(1)}, f32[36,2,256]{2,1,0:T(2,128)S(1)}, u32[]{:S(2)}, u32[]{:S(2)}) collective-permute-start(f32[36,2,256]{2,1,0:T(2,128)S(1)} %get-tuple-element.183), channel_id=1, source_target_pairs={{0,1},{1,2},{2,3},{3,0},{4,5},{5,6},{6,7},{7,4},{8,9},{9,10},{10,1... | collective-permute-start | bytes 221192 | tf_op jit(solution)/shard_map/ppermute | solution.py:31
  492.0 8.4 %copy.367 = f32[3,32,64,256]{3,0,2,1:T(4,128)} copy(f32[3,32,64,256]{3,2,1,0:T(8,128)S(1)} %pad_maximum_fusion) | data formatting | bytes 12582912 | tf_op jit(solution)/shard_map/stack | solution.py:269
  500.4 18.4 %gather_fusion = f32[1024,3]{0,1:T(4,128)S(1)} fusion(f32[3,32,64,256]{3,0,2,1:T(4,128)} %copy.367, s32[1024]{0:T(1024)S(1)} %reshape.934), kind=kCustom, calls=%fused_computation | custom fusion | bytes 36864 | tf_op jit(solution)/shard_map/gather | solution.py:270
  (243 shorter events, 134.5 us)
Async XLA Ops:
  0.0 7.9 %copy-start.26 = (f32[16]{0:T(128)}, f32[16]{0:T(128)S(1)}, u32[]{:S(2)}) copy-start(f32[16]{0:T(128)S(1)} %convert_add_fusion) | copy-start | bytes 196
  0.0 36.7 %copy-start.12 = (f32[132]{0:T(256)}, f32[132]{0:T(256)S(1)}, u32[]{:S(2)}) copy-start(f32[132]{0:T(256)S(1)} %compare_convert_fusion.1) | copy-start | bytes 1588
  5.5 2.1 copy-start.21
  5.6 0.6 copy-start.5
  30.4 32.8 %all-to-all-start = ((f32[4,1,67584]{2,1,0:T(1,128)}), f32[4,1,67584]{2,1,0:T(1,128)S(1)}, u32[]{:S(2)}, u32[]{:S(2)}) async-start(f32[4,1,67584]{2,1,0:T(1,128)} %reshape.1088), calls=%async_computation | async-start | bytes 2162688 | tf_op jit(solution)/shard_map/all_to_all | solution.py:93
  45.8 21.6 %copy-start.19 = (s32[4,2]{0,1:T(2,128)S(1)}, s32[4,2]{0,1:T(2,128)}, u32[]{:S(2)}) copy-start(s32[4,2]{0,1:T(2,128)} %param.13) | copy-start | bytes 100
  45.8 26.8 %copy-start.15 = (s32[3,8]{1,0:T(4,128)S(1)}, s32[3,8]{1,0:T(4,128)}, u32[]{:S(2)}) copy-start(s32[3,8]{1,0:T(4,128)} %param.12) | copy-start | bytes 292
  45.8 26.8 %copy-start.7 = (f32[3,1024]{1,0:T(4,128)S(1)}, f32[3,1024]{1,0:T(4,128)}, u32[]{:S(2)}) copy-start(f32[3,1024]{1,0:T(4,128)} %param.10) | copy-start | bytes 36868
  45.8 26.8 %copy-start.23 = (f32[3]{0:T(128)S(1)}, f32[3]{0:T(128)}, u32[]{:S(2)}) copy-start(f32[3]{0:T(128)} %constant.504.clone) | copy-start | bytes 40
  45.9 33.1 %copy-start.25 = (s32[2,8]{1,0:T(2,128)S(1)}, s32[2,8]{1,0:T(2,128)}, u32[]{:S(2)}) copy-start(s32[2,8]{1,0:T(2,128)} %param.14) | copy-start | bytes 196
  63.1 15.9 %copy-start.1 = (f32[4,1,67584]{2,1,0:T(1,128)}, f32[4,1,67584]{2,1,0:T(1,128)S(1)}, u32[]{:S(2)}) copy-start(f32[4,1,67584]{2,1,0:T(1,128)S(1)} %all-to-all-done) | copy-start | bytes 3244036
  63.1 30.8 %all-to-all-start.1 = ((f32[4,1,67584]{2,1,0:T(1,128)}), f32[4,1,67584]{2,1,0:T(1,128)}, u32[]{:S(2)}, u32[]{:S(2)}) async-start(f32[4,1,67584]{2,1,0:T(1,128)} %reshape.1090), calls=%async_computation.1 | async-start | bytes 2162688 | tf_op jit(solution)/shard_map/all_to_all | solution.py:94
  68.2 282.2 %collective-permute-start.7 = (s32[2]{0:T(128)}, s32[2]{0:T(128)}, u32[]{:S(2)}, u32[]{:S(2)}) collective-permute-start(s32[2]{0:T(128)} %get-tuple-element.157), channel_id=1, source_target_pairs={{0,3},{1,0},{2,1},{3,2},{4,7},{5,4},{6,5},{7,6},{8,11},{9,8},{10,9... | collective-permute-start | bytes 32 | tf_op jit(solution)/shard_map/ppermute | solution.py:21
  72.0 280.4 %collective-permute-start.6 = (s32[2]{0:T(128)}, s32[2]{0:T(128)}, u32[]{:S(2)}, u32[]{:S(2)}) collective-permute-start(s32[2]{0:T(128)} %get-tuple-element.158), channel_id=1, source_target_pairs={{0,1},{1,2},{2,3},{3,0},{4,5},{5,6},{6,7},{7,4},{8,9},{9,10},{10,1... | collective-permute-start | bytes 32 | tf_op jit(solution)/shard_map/ppermute | solution.py:21
  72.0 282.5 %collective-permute-start.5 = (s32[2]{0:T(128)}, s32[2]{0:T(128)}, u32[]{:S(2)}, u32[]{:S(2)}) collective-permute-start(s32[2]{0:T(128)} %get-tuple-element.156), channel_id=1, source_target_pairs={{0,28},{4,0},{8,4},{12,8},{16,12},{20,16},{24,20},{28,24},{1,29},{... | collective-permute-start | bytes 32 | tf_op jit(solution)/shard_map/ppermute | solution.py:21
  72.6 281.9 %collective-permute-start.4 = (s32[2]{0:T(128)}, s32[2]{0:T(128)}, u32[]{:S(2)}, u32[]{:S(2)}) collective-permute-start(s32[2]{0:T(128)} %get-tuple-element.159), channel_id=1, source_target_pairs={{0,4},{4,8},{8,12},{12,16},{16,20},{20,24},{24,28},{28,0},{1,5},{5... | collective-permute-start | bytes 32 | tf_op jit(solution)/shard_map/ppermute | solution.py:21
  73.9 11.3 %copy-start.16 = (s32[2]{0:T(128)}, s32[2]{0:T(128)S(1)}, u32[]{:S(2)}) copy-start(s32[2]{0:T(128)S(1)} %get-tuple-element.215) | copy-start | bytes 28
  75.0 282.2 %collective-permute-start.11 = (f32[2,3,128]{2,1,0:T(4,128)}, f32[2,3,128]{2,1,0:T(4,128)}, u32[]{:S(2)}, u32[]{:S(2)}) collective-permute-start(f32[2,3,128]{2,1,0:T(4,128)} %gather_fusion.9), channel_id=1, source_target_pairs={{0,3},{1,0},{2,1},{3,2},{4,7},{5,4},{6,5},{7,6},{8,11},{9,8},{10,9... | collective-permute-start | bytes 9224 | tf_op jit(solution)/shard_map/ppermute | solution.py:21
  132.3 4.5 copy-start
  132.3 20.9 %all-to-all-start.3 = ((f32[8,1,33792]{2,1,0:T(1,128)}), f32[8,1,33792]{2,1,0:T(1,128)}, u32[]{:S(2)}, u32[]{:S(2)}) async-start(f32[8,1,33792]{2,1,0:T(1,128)} %reshape.1092), calls=%async_computation.3 | async-start | bytes 2162688 | tf_op jit(solution)/shard_map/all_to_all | solution.py:87
  153.2 4.5 copy-start.8
  153.2 4.5 copy-start.24
  153.2 35.6 %all-to-all-start.2 = ((f32[8,1,33792]{2,1,0:T(1,128)}), f32[8,1,33792]{2,1,0:T(1,128)S(1)}, u32[]{:S(2)}, u32[]{:S(2)}) async-start(f32[8,1,33792]{2,1,0:T(1,128)} %reshape.1094), calls=%async_computation.2 | async-start | bytes 2162688 | tf_op jit(solution)/shard_map/all_to_all | solution.py:86
  215.3 2.0 copy-start.2
  238.0 26.6 %all-to-all-start.5 = ((f32[8,1,33792]{2,1,0:T(1,128)}), f32[8,1,33792]{2,1,0:T(1,128)S(1)}, u32[]{:S(2)}, u32[]{:S(2)}) async-start(f32[8,1,33792]{2,1,0:T(1,128)} %reshape.1096), calls=%async_computation.5 | async-start | bytes 2162688 | tf_op jit(solution)/shard_map/all_to_all | solution.py:87
  247.9 0.7 copy-start.3
  264.6 4.7 copy-start.18
  264.6 6.4 %copy-start.14 = (s32[8,4]{0,1:T(4,128)S(1)}, s32[8,4]{0,1:T(4,128)}, u32[]{:S(2)}) copy-start(s32[8,4]{0,1:T(4,128)} %get-tuple-element.208) | copy-start | bytes 388
  264.6 6.5 %copy-start.20 = (s32[4,2]{0,1:T(2,128)S(1)}, s32[4,2]{0,1:T(2,128)}, u32[]{:S(2)}) copy-start(s32[4,2]{0,1:T(2,128)} %param.13) | copy-start | bytes 100
  264.6 36.8 %all-to-all-start.4 = ((f32[8,1,33792]{2,1,0:T(1,128)}), f32[8,1,33792]{2,1,0:T(1,128)}, u32[]{:S(2)}, u32[]{:S(2)}) async-start(f32[8,1,33792]{2,1,0:T(1,128)} %reshape.1098), calls=%async_computation.4 | async-start | bytes 2162688 | tf_op jit(solution)/shard_map/all_to_all | solution.py:86
  345.8 4.4 copy-start.10
  345.8 4.4 copy-start.11
  345.8 4.5 copy-start.6
  345.8 4.5 copy-start.9
  345.8 43.2 %all-to-all-start.7 = ((f32[4,1,67584]{2,1,0:T(1,128)}), f32[4,1,67584]{2,1,0:T(1,128)}, u32[]{:S(2)}, u32[]{:S(2)}) async-start(f32[4,1,67584]{2,1,0:T(1,128)} %reshape.1100), calls=%async_computation.7 | async-start | bytes 2162688 | tf_op jit(solution)/shard_map/all_to_all | solution.py:94
  350.4 22.5 %collective-permute-start.10 = (f32[2,3,128]{2,1,0:T(4,128)S(1)}, f32[2,3,128]{2,1,0:T(4,128)S(1)}, u32[]{:S(2)}, u32[]{:S(2)}) collective-permute-start(f32[2,3,128]{2,1,0:T(4,128)S(1)} %gather_fusion.8), channel_id=1, source_target_pairs={{0,1},{1,2},{2,3},{3,0},{4,5},{5,6},{6,7},{7,4},{8,9},{9,10},{10,1... | collective-permute-start | bytes 9224 | tf_op jit(solution)/shard_map/ppermute | solution.py:21
  352.4 20.5 %collective-permute-start.9 = (f32[2,3,128]{2,1,0:T(4,128)S(1)}, f32[2,3,128]{2,1,0:T(4,128)S(1)}, u32[]{:S(2)}, u32[]{:S(2)}) collective-permute-start(f32[2,3,128]{2,1,0:T(4,128)S(1)} %gather_fusion.7), channel_id=1, source_target_pairs={{0,28},{4,0},{8,4},{12,8},{16,12},{20,16},{24,20},{28,24},{1,29},{... | collective-permute-start | bytes 9224 | tf_op jit(solution)/shard_map/ppermute | solution.py:21
  354.4 18.4 %collective-permute-start.8 = (f32[2,3,128]{2,1,0:T(4,128)S(1)}, f32[2,3,128]{2,1,0:T(4,128)S(1)}, u32[]{:S(2)}, u32[]{:S(2)}) collective-permute-start(f32[2,3,128]{2,1,0:T(4,128)S(1)} %gather_fusion.6), channel_id=1, source_target_pairs={{0,4},{4,8},{8,12},{12,16},{16,20},{20,24},{24,28},{28,0},{1,5},{5... | collective-permute-start | bytes 9224 | tf_op jit(solution)/shard_map/ppermute | solution.py:21
  389.0 47.7 %all-to-all-start.6 = ((f32[4,1,67584]{2,1,0:T(1,128)}), f32[4,1,67584]{2,1,0:T(1,128)}, u32[]{:S(2)}, u32[]{:S(2)}) async-start(f32[4,1,67584]{2,1,0:T(1,128)} %reshape.1102), calls=%async_computation.6 | async-start | bytes 2162688 | tf_op jit(solution)/shard_map/all_to_all | solution.py:93
  395.6 17.3 %copy-start.4 = (f32[2,4,3,128]{3,2,1,0:T(4,128)S(1)}, f32[2,4,3,128]{3,2,1,0:T(4,128)}, u32[]{:S(2)}) copy-start(f32[2,4,3,128]{3,2,1,0:T(4,128)} %copy-done.3) | copy-start | bytes 36868
  395.6 21.4 %copy-start.17 = (s32[2]{0:T(128)S(1)}, s32[2]{0:T(128)}, u32[]{:S(2)}) copy-start(s32[2]{0:T(128)} %copy-done.16) | copy-start | bytes 28
  401.3 4.6 collective-permute-start.12
  402.3 4.0 collective-permute-start.13
  402.4 10.5 %collective-permute-start.14 = (f32[2,3,128]{2,1,0:T(4,128)S(1)}, f32[2,3,128]{2,1,0:T(4,128)S(1)}, u32[]{:S(2)}, u32[]{:S(2)}) collective-permute-start(f32[2,3,128]{2,1,0:T(4,128)S(1)} %get-tuple-element.198), channel_id=1, source_target_pairs={{0,3},{1,0},{2,1},{3,2},{4,7},{5,4},{6,5},{7,6},{8,11},{9,8},{10,9... | collective-permute-start | bytes 9224 | tf_op jit(solution)/shard_map/ppermute | solution.py:21
  406.0 10.9 %collective-permute-start.15 = (f32[2,3,128]{2,1,0:T(4,128)S(1)}, f32[2,3,128]{2,1,0:T(4,128)S(1)}, u32[]{:S(2)}, u32[]{:S(2)}) collective-permute-start(f32[2,3,128]{2,1,0:T(4,128)S(1)} %get-tuple-element.197), channel_id=1, source_target_pairs={{0,1},{1,2},{2,3},{3,0},{4,5},{5,6},{6,7},{7,4},{8,9},{9,10},{10,1... | collective-permute-start | bytes 9224 | tf_op jit(solution)/shard_map/ppermute | solution.py:21
  454.0 1.9 copy-start.13
  471.3 3.2 collective-permute-start
  471.4 6.5 %collective-permute-start.1 = (f32[2,64,256]{2,1,0:T(8,128)S(1)}, f32[2,64,256]{2,1,0:T(8,128)S(1)}, u32[]{:S(2)}, u32[]{:S(2)}) collective-permute-start(f32[2,64,256]{2,1,0:T(8,128)S(1)} %get-tuple-element.184), channel_id=1, source_target_pairs={{0,4},{4,8},{8,12},{12,16},{16,20},{20,24},{24,28},{28,0},{1,5},{5... | collective-permute-start | bytes 393224 | tf_op jit(solution)/shard_map/ppermute | solution.py:31
  477.9 10.7 %collective-permute-start.2 = (f32[36,2,256]{2,1,0:T(2,128)S(1)}, f32[36,2,256]{2,1,0:T(2,128)S(1)}, u32[]{:S(2)}, u32[]{:S(2)}) collective-permute-start(f32[36,2,256]{2,1,0:T(2,128)S(1)} %get-tuple-element.182), channel_id=1, source_target_pairs={{1,0},{2,1},{3,2},{0,3},{5,4},{6,5},{7,6},{4,7},{9,8},{10,9},{11,1... | collective-permute-start | bytes 221192 | tf_op jit(solution)/shard_map/ppermute | solution.py:33
  480.6 9.7 %collective-permute-start.3 = (f32[36,2,256]{2,1,0:T(2,128)S(1)}, f32[36,2,256]{2,1,0:T(2,128)S(1)}, u32[]{:S(2)}, u32[]{:S(2)}) collective-permute-start(f32[36,2,256]{2,1,0:T(2,128)S(1)} %get-tuple-element.183), channel_id=1, source_target_pairs={{0,1},{1,2},{2,3},{3,0},{4,5},{5,6},{6,7},{7,4},{8,9},{9,10},{10,1... | collective-permute-start | bytes 221192 | tf_op jit(solution)/shard_map/ppermute | solution.py:31
  500.3 18.6 %copy-start.22 = (f32[1,1024]{1,0:T(1,128)S(1)}, f32[1,1024]{1,0:T(1,128)}, u32[]{:S(2)}) copy-start(f32[1,1024]{1,0:T(1,128)} %copy-done.21) | copy-start | bytes 12292
  500.3 18.6 %copy-start.27 = (f32[16]{0:T(128)S(1)}, f32[16]{0:T(128)}, u32[]{:S(2)}) copy-start(f32[16]{0:T(128)} %copy-done.26) | copy-start | bytes 196
where the time goes:
time: 531 us; the launch traced here: 520 us
  local copies, waits for them, and re-layouts  267 us (50%)
  other arithmetic  73 us (14%)
  matrix products  65.6 us (12%)
  starting transfers between devices  65.2 us (12%)
  waiting for transfers between devices  48.5 us (9%)
    unnamed x76, local copies, waits for them, and re-layouts  92.6 us
    another operation x12, local copies, waits for them, and re-layouts  46.5 us
    ppermute x12, waiting for transfers between devices, from_behind(): lax.ppermute(shard, axis, [(i, (i + by) % peers) for i in range(peers)])  24.1 us
    all_to_all x3, local copies, waits for them, and re-layouts, turn_wide(): lax.all_to_all(halves[0], 'wide', split_axis=2, concat_axis=3, tiled=True)  19.1 us
    all_to_all x3, local copies, waits for them, and re-layouts, turn_wide(): lax.all_to_all(halves[1], 'wide', split_axis=2, concat_axis=3, tiled=True)  19.1 us
    gather x2, local copies, waits for them, and re-layouts, local(): accel_field[:, cell_x[:, :, None, None], cell_y[:, None, :, None], cell_z...  18.5 us
    all_to_all x2, waiting for transfers between devices, turn_narrow(): lax.all_to_all(halves[0], 'narrow', split_axis=2, concat_axis=3, tiled=True)  17.3 us
    ppermute x12, starting transfers between devices, from_behind(): lax.ppermute(shard, axis, [(i, (i + by) % peers) for i in range(peers)])  16.9 us
  transfers between devices with their start and end apart: 24, of which 9 were waited for; matrix products, arithmetic and copies ran while one was open for 60% of the time, Pallas kernels for 0%

commit v1 on v0

v1 whole, which is shorter than its diff:
```python
import functools
import math

import jax
import jax.numpy as jnp
from jax import lax
from jax.experimental import pallas as pl
from jax.experimental.pallas import tpu as pltpu
from jax.sharding import PartitionSpec as P

G = 256
PX = 2
PY = 4
PZ = 16
PATCH_YZ = PY * PZ
PATCH = PX * PATCH_YZ
SCREEN = 0.5
SOFTEN = 0.5
ERFCX = (
    0.2820947416810428,
    0.28210427504184366,
    0.24651391069954823,
    0.18039116519942175,
    0.058372405908860704,
    0.0792320361696661,
    -0.1983246779625943,
    0.030722780905291756,
    0.06437369661731697,
    -0.025480486181070308,
)
VMEM = pl.BlockSpec(memory_space=pltpu.VMEM)
SMEM = pl.BlockSpec(memory_space=pltpu.SMEM)


def iota(shape, dim):
    return lax.broadcasted_iota(jnp.int32, shape, dim)


def sincos(count):
    quarters = count * (4.0 / G)
    near = jnp.floor(quarters + 0.5)
    z = (quarters - near) * (math.pi / 2)
    q = near.astype(jnp.int32)
    zz = z * z
    c = 1.0 + zz * (-0.5 + zz * (1.0 / 24 + zz * (-1.0 / 720 + zz * (1.0 / 40320))))
    s = z * (1.0 + zz * (-1.0 / 6 + zz * (1.0 / 120 + zz * (-1.0 / 5040))))
    swap = (q & 1) == 1
    cosine = jnp.where(swap, s, c)
    sine = jnp.where(swap, c, s)
    cosine = jnp.where(((q + 1) & 2) == 2, -cosine, cosine)
    sine = jnp.where((q & 2) == 2, -sine, sine)
    return cosine, sine


def split(x):
    hi = x.astype(jnp.bfloat16)
    return hi, (x - hi.astype(jnp.float32)).astype(jnp.bfloat16)


def dot3(left, right, dims=((1,), (0,))):
    dims = (dims, ((), ()))
    dot = functools.partial(
        lax.dot_general, dimension_numbers=dims, preferred_element_type=jnp.float32
    )
    return dot(left[0], right[0]) + (dot(left[0], right[1]) + dot(left[1], right[0]))


def folded(wave):
    return jnp.where(wave > G // 2, wave - G, wave).astype(jnp.float32)


def slope(wave):
    w = wave.astype(jnp.float32)
    return (8.0 * sincos(w)[1] - sincos(2.0 * w)[1]) * (1.0 / 6.0)


def leaf_weights(u):
    members = u.shape[1]
    row = iota((PATCH, members), 0)
    cells = (row // PATCH_YZ, row // PZ % PY, row % PZ)
    product = None
    for c, extent in enumerate((PX, PY, PZ)):
        centre = cells[c].astype(jnp.float32) + 0.5
        coordinate = 0.5 + u[c : c + 1] * (extent - 1.0)
        w = jnp.maximum(0.0, 1.0 - jnp.abs(coordinate - centre))
        product = w if product is None else product * w
    return product


def patch_kernel(fraction, masses, out):
    leaves, members = masses.shape
    m = masses[...]
    for n in range(leaves):
        w = leaf_weights(fraction[:, n * members : (n + 1) * members])
        out[n : n + 1, :] = dot3(split(m), split(w), ((1,), (1,)))[n : n + 1, :]


def mode_columns(base, rows, ny, origin):
    w = base + iota((rows, 1), 0)
    kz = origin[0] + w // ny
    ky = origin[1] + w % ny
    return ky, kz


def forward_kernel(ny, chunk, origin, patches, cells, out, e_hi, e_lo):
    step = pl.program_id(0)
    size = patches.shape[0]
    modes = out.shape[0]
    x_col = patches[:, PATCH : PATCH + 1]
    kx = iota((size, G), 1).astype(jnp.float32)
    for a in range(PX):
        c, s = sincos((x_col + float(a)) * kx)
        r0, r1 = a * size, (PX + a) * size
        for part, r, col in ((c, r0, 0), (-s, r0, G), (s, r1, 0), (c, r1, G)):
            hi, lo = split(part)
            e_hi[r : r + size, col : col + G] = hi
            e_lo[r : r + size, col : col + G] = lo
    y_row = cells[1:2, :]
    z_row = cells[2:3, :]

    def body(i, carry):
        at = pl.ds(pl.multiple_of(i * chunk, 8), chunk)
        ky, kz = mode_columns(i * chunk, chunk, ny, origin)
        kyf, kzf = ky.astype(jnp.float32), kz.astype(jnp.float32)
        lane = iota((1, PATCH_YZ), 1)
        tc, ts = sincos(
            kyf * (lane // PZ).astype(jnp.float32) + kzf * (lane % PZ).astype(jnp.float32)
        )
        tc, ts = split(tc), split(ts)
        c, s = sincos(kyf * y_row + kzf * z_row)
        real, imag = [], []
        for a in range(PX):
            p = split(patches[:, a * PATCH_YZ : (a + 1) * PATCH_YZ])
            fc = dot3(tc, p, ((1,), (1,)))
            fs = dot3(ts, p, ((1,), (1,)))
            real.append(fc * c - fs * s)
            imag.append(-(fc * s + fs * c))
        m = split(jnp.concatenate(real + imag, axis=1))
        got = dot3(m, (e_hi[...], e_lo[...]))

        @pl.when(step == 0)
        def _():
            out[at, :] = got

        @pl.when(step > 0)
        def _():
            out[at, :] += got

        @pl.when(step == pl.num_programs(0) - 1)
        def _():
            unit = 2.0 * math.pi / G
            fx = folded(iota((1, G), 1)) * unit
            fy, fz = folded(ky) * unit, folded(kz) * unit
            total = fx * fx + (fy * fy + fz * fz)
            divisor = jnp.where(total > 0, total, 1.0)
            green = jnp.where(
                total > 0, -4.0 * math.pi * jnp.exp(-total * (SCREEN * SCREEN)) / divisor, 0.0
            )
            for col in (0, G):
                out[at, col : col + G] = out[at, col : col + G] * green

        return carry

    lax.fori_loop(0, modes // chunk, body, 0)


def inverse_kernel(ny, chunk, origin, spectrum, cells, out, e_hi, e_lo, acc):
    size = cells.shape[1]
    modes = spectrum.shape[0]
    width = PX * size
    kx = iota((G, size), 0).astype(jnp.float32)
    for a in range(PX):
        c, s = sincos((cells[0:1, :] + float(a)) * kx)
        c0, c1 = a * size, (PX + a) * size
        for part, r, col in ((c, 0, c0), (s, 0, c1), (-s, G, c0), (c, G, c1)):
            hi, lo = split(part)
            e_hi[r : r + G, col : col + size] = hi
            e_lo[r : r + G, col : col + size] = lo
    y_row = cells[1:2, :]
    z_row = cells[2:3, :]
    acc[...] = jnp.zeros_like(acc)

    def body(i, carry):
        at = pl.ds(pl.multiple_of(i * chunk, 8), chunk)
        ky, kz = mode_columns(i * chunk, chunk, ny, origin)
        c, s = sincos(ky.astype(jnp.float32) * y_row + kz.astype(jnp.float32) * z_row)
        spec = spectrum[at, :]
        e = (e_hi[...], e_lo[...])
        lane_w = i * chunk + iota((1, chunk), 1)
        kz_row = origin[0] + lane_w // ny
        ky_row = origin[1] + lane_w % ny
        row = iota((PATCH_YZ, 1), 0)
        tc, ts = sincos(
            ky_row.astype(jnp.float32) * (row // PZ).astype(jnp.float32)
            + kz_row.astype(jnp.float32) * (row % PZ).astype(jnp.float32)
        )
        half = G // 2
        weight = jnp.where(
            (kz_row == 0) | (kz_row == half), 1.0, jnp.where(kz_row < half, 2.0, 0.0)
        ) * (1.0 / float(G * G * G))
        tc, ts = tc * weight, ts * weight
        dy, dz = slope(ky_row), slope(kz_row)

        def fields(source, cos_rows, sin_rows):
            p = dot3(split(source), e)
            total = None
            real, imag = [], []
            for a in range(PX):
                pr = p[:, a * size : (a + 1) * size]
                pi = p[:, (PX + a) * size : (PX + a + 1) * size]
                real.append(pr * c - pi * s)
                imag.append(pr * s + pi * c)
            real = split(jnp.concatenate(real, axis=1))
            imag = split(jnp.concatenate(imag, axis=1))
            return dot3(split(sin_rows), real) + dot3(split(cos_rows), imag)

        dx = slope(iota((1, 2 * G), 1) % G)
        acc[0:PATCH_YZ, :] += fields(spec * dx, tc, ts)
        acc[PATCH_YZ:, :] += fields(
            spec,
            jnp.concatenate([tc * dy, tc * dz], axis=0),
            jnp.concatenate([ts * dy, ts * dz], axis=0),
        )
        return carry

    lax.fori_loop(0, modes // chunk, body, 0)
    for f in range(3):
        for a in range(PX):
            block = acc[f * PATCH_YZ : (f + 1) * PATCH_YZ, a * size : (a + 1) * size]
            col = f * PATCH + a * PATCH_YZ
            out[:, col : col + PATCH_YZ] = block.T


def pair_kernel(leaves, jobs, source_at, target_at, shift, live, sources, out):
    out[...] = jnp.zeros_like(out)

    def body(j, carry):
        target = target_at[j]
        tgt = sources[target]
        total = [0.0, 0.0, 0.0]
        for k in range(2):
            src = sources[source_at[k, j]]
            cols = src.T
            members = src.shape[1]
            d = []
            for c in range(3):
                col = cols[:, c : c + 1] + shift[3 * k + c, j]
                d.append(jnp.broadcast_to(col, (members, members)) - tgt[c : c + 1, :])
            squared = d[0] * d[0] + d[1] * d[1] + d[2] * d[2]
            r = squared * lax.rsqrt(jnp.maximum(squared, 1e-30))
            t = 1.0 / (1.0 + 0.5 * r)
            poly = ERFCX[-1] * t + ERFCX[-2]
            for coefficient in ERFCX[-3::-1]:
                poly = poly * t + coefficient
            screened = jnp.exp(-squared) * (poly * t + (2.0 / math.sqrt(math.pi)) * r)
            inv = lax.rsqrt(squared + SOFTEN * SOFTEN)
            w = cols[:, 3:4] * screened * (inv * inv * inv)
            for c in range(3):
                total[c] = total[c] + jnp.sum(w * d[c], axis=0, keepdims=True)
        pick = live[j]
        out[target, 0:3, :] += jnp.concatenate(total, axis=0) * pick
        return carry

    lax.fori_loop(0, jobs, body, 0)


def sample_kernel(field, fraction, short, out):
    leaves = field.shape[0]
    members = fraction.shape[1] // leaves
    for n in range(leaves):
        at = slice(n * members, (n + 1) * members)
        w = split(leaf_weights(fraction[:, at]))
        values = jnp.concatenate(
            [field[n : n + 1, f * PATCH : (f + 1) * PATCH] for f in range(3)], axis=0
        )
        out[:, at] = dot3(split(values), w) + short[n, 0:3, :]


def local(fraction, masses, leaf_cell, exports, tile_lists):
    leaves = leaf_cell.shape[1]
    members = masses.shape[0] // leaves
    slots = exports.shape[1]
    n_wide, n_narrow = lax.axis_size("wide"), lax.axis_size("narrow")
    everyone = ("wide", "narrow")
    total = leaves * n_wide * n_narrow
    leaf_mass = masses.reshape(leaves, members)
    f32 = jnp.float32

    patch = pl.pallas_call(
        patch_kernel,
        out_shape=jax.ShapeDtypeStruct((leaves, PATCH), f32),
        in_specs=[VMEM, VMEM],
        out_specs=VMEM,
        name="patch",
    )(fraction, leaf_mass)
    cell_f = leaf_cell.astype(f32)
    packed = jnp.concatenate([patch, cell_f.T], axis=1)
    gathered = lax.all_gather(packed, everyone, axis=0, tiled=True)
    cells = gathered[:, PATCH : PATCH + 3].T

    extents = jnp.asarray([PX - 1.0, PY - 1.0, PZ - 1.0], dtype=f32)
    place = fraction.reshape(3, leaves, members) * extents[:, None, None] + 0.5
    place = jnp.transpose(cell_f[:, :, None] + place, (1, 0, 2))
    notes = jnp.concatenate([tile_lists.T.astype(f32), cell_f.T], axis=1)
    notes = jnp.pad(notes, ((0, 0), (0, members - notes.shape[1])))
    book = jnp.concatenate([place, leaf_mass[:, None], notes[:, None]], axis=1)
    books = [book]
    for axis, by in (("wide", -1), ("wide", 1), ("narrow", -1), ("narrow", 1)):
        peers = lax.axis_size(axis)
        books.append(lax.ppermute(book, axis, [(i, (i + by) % peers) for i in range(peers)]))
    books = jnp.stack(books)
    lists = books[:, :, 4, 0:2].astype(jnp.int32)
    corner = books[:, :, 4, 2:5]
    chosen = jnp.minimum(exports, leaves - 1).reshape(-1)
    target_at = jnp.concatenate([jnp.arange(leaves, dtype=jnp.int32), chosen])
    rank_at = jnp.concatenate(
        [jnp.zeros((leaves,), jnp.int32), jnp.repeat(jnp.arange(1, 5, dtype=jnp.int32), slots)]
    )
    live = jnp.concatenate([jnp.ones((leaves,), f32), (exports < leaves).astype(f32).reshape(-1)])
    source_at = rank_at[None, :] * leaves + lists[rank_at, target_at].T
    apart = corner.reshape(5 * leaves, 3)[source_at] - cell_f.T[target_at][None]
    shift = -float(G) * jnp.floor(apart / G + 0.5)
    shift = jnp.transpose(shift, (0, 2, 1)).reshape(6, -1)
    jobs = target_at.shape[0]
    sources = jnp.pad(books.reshape(5 * leaves, 5, members), ((0, 0), (0, 3), (0, 0)))
    short = pl.pallas_call(
        functools.partial(pair_kernel, leaves, jobs),
        out_shape=jax.ShapeDtypeStruct((leaves, 8, members), f32),
        in_specs=[SMEM, SMEM, SMEM, SMEM, VMEM],
        out_specs=VMEM,
        cost_estimate=pl.CostEstimate(
            flops=jobs * 2 * members * members * 60, bytes_accessed=2**20, transcendentals=0
        ),
        name="pairs",
    )(source_at, target_at, shift, live, sources)

    nz = -(-(G // 2 + 1) // n_narrow)
    ny = G // n_wide
    modes = nz * ny
    parts = next(p for p in range(1, modes + 1) if nz % p == 0 and modes // p <= 384)
    chunk = modes // parts
    origin = jnp.stack([lax.axis_index("narrow") * nz, lax.axis_index("wide") * ny]).astype(
        jnp.int32
    )
    size = min(total, 256)
    blocks = total // size
    params = pltpu.CompilerParams(vmem_limit_bytes=56 * 2**20)
    spectrum = pl.pallas_call(
        functools.partial(forward_kernel, ny, chunk),
        grid=(blocks,),
        out_shape=jax.ShapeDtypeStruct((modes, 2 * G), f32),
        in_specs=[
            SMEM,
            pl.BlockSpec((size, PATCH + 3), lambda i: (i, 0)),
            pl.BlockSpec((3, size), lambda i: (0, i)),
        ],
        out_specs=pl.BlockSpec((modes, 2 * G), lambda i: (0, 0)),
        scratch_shapes=[
            pltpu.VMEM((2 * PX * size, 2 * G), jnp.bfloat16),
            pltpu.VMEM((2 * PX * size, 2 * G), jnp.bfloat16),
        ],
        compiler_params=params,
        name="forward",
    )(origin, gathered, cells)
    partial = pl.pallas_call(
        functools.partial(inverse_kernel, ny, chunk),
        grid=(blocks,),
        out_shape=jax.ShapeDtypeStruct((total, 3 * PATCH), f32),
        in_specs=[
            SMEM,
            pl.BlockSpec((modes, 2 * G), lambda i: (0, 0)),
            pl.BlockSpec((3, size), lambda i: (0, i)),
        ],
        out_specs=pl.BlockSpec((size, 3 * PATCH), lambda i: (i, 0)),
        scratch_shapes=[
            pltpu.VMEM((2 * G, 2 * PX * size), jnp.bfloat16),
            pltpu.VMEM((2 * G, 2 * PX * size), jnp.bfloat16),
            pltpu.VMEM((3 * PATCH_YZ, PX * size), f32),
        ],
        compiler_params=params,
        name="inverse",
    )(origin, spectrum, cells)
    field = lax.psum_scatter(partial, everyone, scatter_dimension=0, tiled=True)
    return pl.pallas_call(
        sample_kernel,
        out_shape=jax.ShapeDtypeStruct((3, leaves * members), f32),
        in_specs=[VMEM, VMEM, VMEM],
        out_specs=VMEM,
        name="sample",
    )(field, fraction, short)


def solution(mesh):
    placed = (
        P(None, ("wide", "narrow")),
        P(("wide", "narrow")),
        P(None, ("wide", "narrow")),
        P(None, ("wide", "narrow")),
        P(None, ("wide", "narrow")),
    )
    return jax.shard_map(
        local, mesh=mesh, in_specs=placed, out_specs=P(None, ("wide", "narrow")), check_vma=False
    )
```

time: 531 us -> 255 us (0.48); the launches traced: 520 us -> 254 us
  local copies, waits for them, and re-layouts: 267 us -> 7.66 us
  blocking collectives: 0 us -> 70.8 us
  other arithmetic: 73 us -> 4.87 us
  matrix products: 65.6 us -> 0 us
  waiting for transfers between devices: 48.5 us -> 111 us
  starting transfers between devices: 65.2 us -> 6.97 us
  Pallas kernels: 0 us -> 39.5 us
  between operations: 1.29 us -> 13.5 us
    unnamed x0 -> x2, waiting for transfers between devices: none -> 111 us
    unnamed x76 -> x13, local copies, waits for them, and re-layouts: 92.6 us -> 3.51 us
    all_gather x0 -> x1, blocking collectives: none -> 70.8 us  [local(): gathered = lax.all_gather(packed, everyone, axis=0, tiled=True)]
    dot_general x22 -> x0, matrix products: 65.6 us -> none  [the longest x3 9.21 us: forward(): result_imag = -jnp.einsum(pattern, real_part, sine_table, precision=PRECISE)]
    another operation x13 -> x3, local copies, waits for them, and re-layouts: 54.8 us -> 0.11 us  [the longest x1 0.07 us: local(): apart = corner.reshape(5 * leaves, 3)[source_at] - cell_f.T[target_at][None]]
    all_to_all x11 -> x0, local copies, waits for them, and re-layouts: 53.2 us -> none  [the longest x3 19.1 us: turn_wide(): lax.all_to_all(halves[0], 'wide', split_axis=2, concat_axis=3, tiled=True)]
    pallas_call x0 -> x5, Pallas kernels: none -> 39.5 us  [the longest x1 16.5 us: local(): pl.pallas_call(functools.partial(inverse_kernel, ny, chunk), grid=(blocks...]
    all_to_all x8 -> x0, starting transfers between devices: 39.3 us -> none  [the longest x2 12.9 us: turn_narrow(): lax.all_to_all(halves[0], 'narrow', split_axis=2, concat_axis=3, tiled=True)]
  transfers between devices with their start and end apart: 24 -> 5, of which waited for: 9 -> 1; matrix products, arithmetic and copies ran while one was open for 60% -> 3% of each run, Pallas kernels for 0% -> 15%
where the time goes in v1:
time: 255 us; the launch traced here: 254 us
  waiting for transfers between devices  111 us (44%)
  blocking collectives  70.8 us (28%)
  Pallas kernels  39.5 us (15%)
  between operations  13.5 us (5%)
  local copies, waits for them, and re-layouts  7.66 us (3%)
  starting transfers between devices  6.97 us (3%)
  other arithmetic  4.87 us (2%)
    unnamed x2, waiting for transfers between devices  111 us
    all_gather x1, blocking collectives, local(): gathered = lax.all_gather(packed, everyone, axis=0, tiled=True)  70.8 us
    pallas_call x1, Pallas kernels, local(): pl.pallas_call(functools.partial(inverse_kernel, ny, chunk), grid=(blocks...  16.5 us
    pallas_call x1, Pallas kernels, local(): pl.pallas_call(functools.partial(forward_kernel, ny, chunk), grid=(blocks...  10.9 us
    pallas_call x1, Pallas kernels, local(): pl.pallas_call(functools.partial(pair_kernel, leaves, jobs), out_shape=ja...  8.32 us
    ppermute x4, starting transfers between devices, local(): lax.ppermute(book, axis, [(i, (i + by) % peers) for i in range(peers)])  6.97 us
  transfers between devices with their start and end apart: 5, of which 1 were waited for; matrix products, arithmetic and copies ran while one was open for 3% of the time, Pallas kernels for 15%

profile of v1, /device:TPU:0, one launch (start us, length us, event | category | flops | bytes accessed | tf_op | source)
XLA Modules:
  0.0 254.0 jit_solution(16331502531812176280)
XLA Ops:
  6.5 0.0 all-reduce.7.cloned.1.call-start
  6.5 0.8 copy.46
  7.3 0.8 copy.49
  8.1 0.1 copy.48
  8.1 0.1 fusion.4
  8.2 0.8 fusion.3
  9.0 0.7 pad_maximum_fusion
  9.7 3.4 %collective-permute-start = (f32[8,5,128]{2,0,1:T(8,128)S(1)}, f32[8,5,128]{2,0,1:T(8,128)S(1)}, u32[]{:S(2)}, u32[]{:S(2)}) collective-permute-start(f32[8,5,128]{2,0,1:T(8,128)S(1)} %pad_maximum_fusion), channel_id=1, source_target_pairs={{0,28},{4,0},{8,4},{12,8},{16,12},{20,16},{24,20},{28,24},{1,29},{... | collective-permute-start | bytes 61448 | tf_op jit(solution)/shard_map/ppermute | solution.py:310
  13.1 0.0 collective-permute-start.1
  13.1 3.6 %collective-permute-start.2 = (f32[8,5,128]{2,0,1:T(8,128)S(1)}, f32[8,5,128]{2,0,1:T(8,128)S(1)}, u32[]{:S(2)}, u32[]{:S(2)}) collective-permute-start(f32[8,5,128]{2,0,1:T(8,128)S(1)} %pad_maximum_fusion), channel_id=1, source_target_pairs={{0,3},{1,0},{2,1},{3,2},{4,7},{5,4},{6,5},{7,6},{8,11},{9,8},{10,9... | collective-permute-start | bytes 61448 | tf_op jit(solution)/shard_map/ppermute | solution.py:310
  16.7 0.0 collective-permute-start.3
  16.7 1.9 patch.1
  18.6 0.7 pad_maximum_fusion.1
  19.3 70.8 %all_gather.3.patches = f32[256,131]{1,0:T(8,128)S(1)} all-gather(f32[8,131]{1,0:T(8,128)S(1)} %pad_maximum_fusion.1), channel_id=1, replica_groups=mesh['wide'=8,'narrow'=4] {'wide','narrow'}, dimensions={0}, use_global_device_ids=true | all-gather | bytes 138336 | tf_op jit(solution)/shard_map/all_gather | solution.py:298
  90.0 0.0 copy-start
  90.0 0.7 copy.65
  90.7 0.7 pad_add_fusion.origin
  91.4 0.0 copy-done
  91.4 0.0 copy-start.1
  91.4 0.0 copy-start.2
  91.4 10.9 %forward.1.spectrum = f32[1056,512]{1,0:T(8,128)} custom-call(s32[2]{0:T(128)} %pad_add_fusion.origin, f32[256,131]{1,0:T(8,128)} %copy-done, f32[3,256]{1,0:T(4,128)} %bitcast.64), custom_call_target="tpu_custom_call" | custom-call | tf_op jit(solution)/shard_map/forward/pallas_call | solution.py:348
  102.2 16.5 %inverse.1 = f32[256,384]{1,0:T(8,128)} custom-call(s32[2]{0:T(128)} %pad_add_fusion.origin, f32[1056,512]{1,0:T(8,128)} %forward.1.spectrum, f32[3,256]{1,0:T(4,128)} %bitcast.65), custom_call_target="tpu_custom_call" | custom-call | tf_op jit(solution)/shard_map/inverse/pallas_call | solution.py:365
  118.8 0.0 all-reduce.7.cloned.1.call-update
  118.8 0.0 copy-done.1
  118.8 0.0 copy-done.2
  118.8 0.1 copy.51
  118.9 0.1 concatenate.50
  119.0 0.1 reshape.97
  119.1 0.1 broadcast_in_dim.8
  119.2 0.1 reshape.95
  119.3 0.1 pad_multiply_fusion
  119.3 0.1 copy.60
  119.5 0.1 reshape.99
  119.5 0.6 pad_convert_fusion.live
  120.2 0.1 fusion.13
  120.3 0.6 pad_add_fusion.1.target_at
  120.8 0.0 collective-permute-done
  120.8 0.0 collective-permute-done.1
  120.8 0.0 collective-permute-done.2
  120.9 0.0 collective-permute-done.3
  120.9 0.1 slice_bitcast_fusion
  121.0 0.6 gather_fusion
  121.6 0.1 copy.53
  121.7 0.6 compare_select_fusion
  122.3 0.1 reshape.109
  122.4 0.6 gather_fusion.1
  122.9 0.1 copy.64
  123.0 0.6 gather_fusion.2
  123.6 0.1 copy.58
  123.7 0.6 reshape.98.shift
  124.3 0.7 pad.12.sources
  125.0 8.3 %pairs.1.short = f32[8,8,128]{2,1,0:T(8,128)} custom-call(s32[2,16]{1,0:T(2,128)} %get-tuple-element.6.source_at, s32[16]{0:T(128)} %pad_add_fusion.1.target_at, f32[6,16]{1,0:T(8,128)} %reshape.98.shift, f32[16]{0:T(128)} %pad_convert_fusion.live, f32[40,8,128]{2,1,0:T(8,128)} %pad.12.sources), custom_call_target="tpu_custom_call" | custom-call | flops 31457280 | bytes 1048576 | tf_op jit(solution)/shard_map/pairs/pallas_call | solution.py:326
  133.3 110.7 %all-reduce.7.cloned.1.call-done = f32[256,384]{1,0:T(8,128)} async-done(((f32[256,384]{1,0:T(8,128)}), f32[256,384]{1,0:T(8,128)}) %all-reduce.7.cloned.1.call-update) | async-done | bytes 393232
  244.0 1.3 constant_dynamic-slice_fusion.field
  245.3 1.9 sample.1
  (18 shorter events, 0.1 us)
Async XLA Ops:
  6.5 237.4 %all-reduce.7.cloned.1.call-start = ((), (), s32[]{:S(2)}) async-start(), calls=%async_computation | async-start | bytes 786432
  9.7 111.1 %collective-permute-start = (f32[8,5,128]{2,0,1:T(8,128)S(1)}, f32[8,5,128]{2,0,1:T(8,128)S(1)}, u32[]{:S(2)}, u32[]{:S(2)}) collective-permute-start(f32[8,5,128]{2,0,1:T(8,128)S(1)} %pad_maximum_fusion), channel_id=1, source_target_pairs={{0,28},{4,0},{8,4},{12,8},{16,12},{20,16},{24,20},{28,24},{1,29},{... | collective-permute-start | bytes 61448 | tf_op jit(solution)/shard_map/ppermute | solution.py:310
  13.1 107.8 %collective-permute-start.1 = (f32[8,5,128]{2,0,1:T(8,128)S(1)}, f32[8,5,128]{2,0,1:T(8,128)S(1)}, u32[]{:S(2)}, u32[]{:S(2)}) collective-permute-start(f32[8,5,128]{2,0,1:T(8,128)S(1)} %pad_maximum_fusion), channel_id=1, source_target_pairs={{0,4},{4,8},{8,12},{12,16},{16,20},{20,24},{24,28},{28,0},{1,5},{5... | collective-permute-start | bytes 61448 | tf_op jit(solution)/shard_map/ppermute | solution.py:310
  13.1 107.8 %collective-permute-start.2 = (f32[8,5,128]{2,0,1:T(8,128)S(1)}, f32[8,5,128]{2,0,1:T(8,128)S(1)}, u32[]{:S(2)}, u32[]{:S(2)}) collective-permute-start(f32[8,5,128]{2,0,1:T(8,128)S(1)} %pad_maximum_fusion), channel_id=1, source_target_pairs={{0,3},{1,0},{2,1},{3,2},{4,7},{5,4},{6,5},{7,6},{8,11},{9,8},{10,9... | collective-permute-start | bytes 61448 | tf_op jit(solution)/shard_map/ppermute | solution.py:310
  16.7 104.2 %collective-permute-start.3 = (f32[8,5,128]{2,0,1:T(8,128)S(1)}, f32[8,5,128]{2,0,1:T(8,128)S(1)}, u32[]{:S(2)}, u32[]{:S(2)}) collective-permute-start(f32[8,5,128]{2,0,1:T(8,128)S(1)} %pad_maximum_fusion), channel_id=1, source_target_pairs={{0,1},{1,2},{2,3},{3,0},{4,5},{5,6},{6,7},{7,4},{8,9},{9,10},{10,1... | collective-permute-start | bytes 61448 | tf_op jit(solution)/shard_map/ppermute | solution.py:310
  90.0 1.3 copy-start
  91.4 27.4 %copy-start.1 = (f32[1024]{0:T(1024)S(1)}, f32[1024]{0:T(1024)}, u32[]{:S(2)}) copy-start(f32[1024]{0:T(1024)} %param.7) | copy-start | bytes 12292
  91.4 27.5 %copy-start.2 = (s32[4,2]{0,1:T(2,128)S(1)}, s32[4,2]{0,1:T(2,128)}, u32[]{:S(2)}) copy-start(s32[4,2]{0,1:T(2,128)} %param.9) | copy-start | bytes 100
Sparse Core Ops, SparseCore 0:
  118.9 125.0 all-reduce.6

commit v2 on v1

--- a/solution.py
+++ b/solution.py
@@ -87,12 +87,142 @@
     return product
 
 
-def patch_kernel(fraction, masses, out):
-    leaves, members = masses.shape
-    m = masses[...]
+def pack_kernel(leaf_cell, tile_lists, fraction, masses, packed, book):
+    leaves = packed.shape[0]
+    members = masses.shape[1] // leaves
+    lane = iota((1, members), 1)
     for n in range(leaves):
-        w = leaf_weights(fraction[:, n * members : (n + 1) * members])
-        out[n : n + 1, :] = dot3(split(m), split(w), ((1,), (1,)))[n : n + 1, :]
+        at = slice(n * members, (n + 1) * members)
+        u = fraction[:, at]
+        m = masses[:, at]
+        w = leaf_weights(u)
+        full = jnp.broadcast_to(m, (8, members))
+        packed[n : n + 1, 0:PATCH] = dot3(split(full), split(w), ((1,), (1,)))[0:1, :]
+        cell = [leaf_cell[c, n].astype(jnp.float32) for c in range(3)]
+        note = jnp.zeros((1, members), jnp.float32)
+        for c in range(3):
+            note = jnp.where(lane == c, cell[c], note)
+        packed[n : n + 1, PATCH:] = note[:, 0:PATCH]
+        for k in range(2):
+            note = jnp.where(lane == 3 + k, tile_lists[k, n].astype(jnp.float32), note)
+        for c, extent in enumerate((PX, PY, PZ)):
+            book[n, c : c + 1, :] = cell[c] + (u[c : c + 1] * (extent - 1.0) + 0.5)
+        book[n, 3:4, :] = m
+        book[n, 4:5, :] = note
+        book[n, 5:8, :] = jnp.zeros((3, members), jnp.float32)
+
+
+def peers_of(axis):
+    count = lax.axis_size(axis)
+    me = lax.axis_index(axis)
+    return [(axis, s, lax.rem(me + s, count), lax.rem(me + count - s, count)) for s in range(1, count)]
+
+
+def greet(groups):
+    barrier = pltpu.get_barrier_semaphore()
+    for axis, _, ahead, _ in groups:
+        pl.semaphore_signal(
+            barrier, inc=1, device_id={axis: ahead}, device_id_type=pl.DeviceIdType.MESH
+        )
+    pl.semaphore_wait(barrier, len(groups))
+
+
+def remote(src, dst, send, recv, axis, to):
+    return pltpu.make_async_remote_copy(
+        src_ref=src,
+        dst_ref=dst,
+        send_sem=send,
+        recv_sem=recv,
+        device_id={axis: to},
+        device_id_type=pl.DeviceIdType.MESH,
+    )
+
+
+def gather_kernel(packed, book, out, books, own, sends, recvs):
+    wide, narrow = peers_of("wide"), peers_of("narrow")
+    w, v = lax.axis_index("wide"), lax.axis_index("narrow")
+    keep = [
+        pltpu.make_async_copy(packed, out.at[w, v], own.at[0]),
+        pltpu.make_async_copy(book, books.at[0], own.at[1]),
+    ]
+    for copy in keep:
+        copy.start()
+    greet(wide + narrow)
+    at = 0
+    first = []
+    for axis, s, ahead, _ in narrow:
+        first.append(remote(packed, out.at[w, v], sends.at[at], recvs.at[at], axis, ahead))
+        at += 1
+    for copy in first:
+        copy.start()
+    near = []
+    for slot, (axis, to) in enumerate(
+        (
+            ("wide", wide[-1][2]),
+            ("wide", wide[0][2]),
+            ("narrow", narrow[-1][2]),
+            ("narrow", narrow[0][2]),
+        )
+    ):
+        near.append(remote(book, books.at[slot + 1], sends.at[at], recvs.at[at], axis, to))
+        at += 1
+    for copy in keep:
+        copy.wait()
+    for copy, (axis, s, _, behind) in zip(first, narrow):
+        remote(
+            packed, out.at[w, behind], sends.at[s - 1], recvs.at[s - 1], axis, behind
+        ).wait_recv()
+    second = []
+    base = at
+    for axis, s, ahead, _ in wide:
+        second.append(remote(out.at[w], out.at[w], sends.at[at], recvs.at[at], axis, ahead))
+        at += 1
+    for copy in second + near:
+        copy.start()
+    for axis, s, _, behind in wide:
+        i = base + s - 1
+        remote(out.at[w], out.at[behind], sends.at[i], recvs.at[i], axis, behind).wait_recv()
+    for copy in near:
+        copy.wait_recv()
+    for copy in first + second + near:
+        copy.wait_send()
+
+
+def scatter_kernel(partial, out, landed, mine, near, sends, recvs):
+    wide, narrow = peers_of("wide"), peers_of("narrow")
+    w, v = lax.axis_index("wide"), lax.axis_index("narrow")
+    greet(wide + narrow)
+    at = 0
+    first = []
+    for axis, s, ahead, _ in wide:
+        first.append(
+            remote(partial.at[ahead], landed.at[s - 1], sends.at[at], recvs.at[at], axis, ahead)
+        )
+        at += 1
+    for copy in first:
+        copy.start()
+    for copy in first:
+        copy.wait_recv()
+    total = partial[w]
+    for s in range(len(wide)):
+        total = total + landed[s]
+    mine[...] = total
+    second = []
+    for axis, s, ahead, _ in narrow:
+        second.append(
+            remote(mine.at[ahead], near.at[s - 1], sends.at[at], recvs.at[at], axis, ahead)
+        )
+        at += 1
+    for copy in second:
+        copy.start()
+    for copy in second:
+        copy.wait_recv()
+    total = mine[v]
+    for s in range(len(narrow)):
+        total = total + near[s]
+    out[...] = total
+    for copy in first + second:
+        copy.wait_send()
 
 
 def mode_columns(base, rows, ny, origin):
@@ -102,7 +232,7 @@
     return ky, kz
 
 
-def forward_kernel(ny, chunk, origin, patches, cells, out, e_hi, e_lo):
+def forward_kernel(ny, chunk, origin, patches, out, e_hi, e_lo):
     step = pl.program_id(0)
     size = patches.shape[0]
     modes = out.shape[0]
@@ -115,6 +245,7 @@
             hi, lo = split(part)
             e_hi[r : r + size, col : col + G] = hi
             e_lo[r : r + size, col : col + G] = lo
+    cells = patches[:, PATCH:].T
     y_row = cells[1:2, :]
     z_row = cells[2:3, :]
 
@@ -164,8 +295,9 @@
     lax.fori_loop(0, modes // chunk, body, 0)
 
 
-def inverse_kernel(ny, chunk, origin, spectrum, cells, out, e_hi, e_lo, acc):
-    size = cells.shape[1]
+def inverse_kernel(ny, chunk, origin, spectrum, leaf_rows, out, e_hi, e_lo, acc):
+    size = leaf_rows.shape[0]
+    cells = leaf_rows[:, PATCH:].T
     modes = spectrum.shape[0]
     width = PX * size
     kx = iota((G, size), 0).astype(jnp.float32)
@@ -231,20 +363,22 @@
             out[:, col : col + PATCH_YZ] = block.T
 
 
-def pair_kernel(leaves, jobs, source_at, target_at, shift, live, sources, out):
+def pair_kernel(leaves, slots, exports, notes, books, out):
     out[...] = jnp.zeros_like(out)
 
-    def body(j, carry):
-        target = target_at[j]
-        tgt = sources[target]
+    def job(rank, target, pick):
+        tgt = books[0, target]
         total = [0.0, 0.0, 0.0]
         for k in range(2):
-            src = sources[source_at[k, j]]
+            source = notes[rank, target, 3 + k]
+            src = books[rank, source]
             cols = src.T
             members = src.shape[1]
             d = []
             for c in range(3):
-                col = cols[:, c : c + 1] + shift[3 * k + c, j]
+                apart = (notes[rank, source, c] - notes[0, target, c]).astype(jnp.float32)
+                wraps = (apart > 0.5 * G).astype(jnp.int32) - (apart <= -0.5 * G).astype(jnp.int32)
+                col = cols[:, c : c + 1] - float(G) * wraps.astype(jnp.float32)
                 d.append(jnp.broadcast_to(col, (members, members)) - tgt[c : c + 1, :])
             squared = d[0] * d[0] + d[1] * d[1] + d[2] * d[2]
             r = squared * lax.rsqrt(jnp.maximum(squared, 1e-30))
@@ -257,11 +391,20 @@
             w = cols[:, 3:4] * screened * (inv * inv * inv)
             for c in range(3):
                 total[c] = total[c] + jnp.sum(w * d[c], axis=0, keepdims=True)
-        pick = live[j]
         out[target, 0:3, :] += jnp.concatenate(total, axis=0) * pick
+
+    def own(n, carry):
+        job(0, n, 1.0)
         return carry
 
-    lax.fori_loop(0, jobs, body, 0)
+    def guest(j, carry):
+        face = j // slots
+        leaf = exports[face, j % slots]
+        job(face + 1, jnp.minimum(leaf, leaves - 1), (leaf < leaves).astype(jnp.float32))
+        return carry
+
+    lax.fori_loop(0, leaves, own, 0)
+    lax.fori_loop(0, 4 * slots, guest, 0)
 
 
 def sample_kernel(field, fraction, short, out):
@@ -281,58 +424,45 @@
     members = masses.shape[0] // leaves
     slots = exports.shape[1]
     n_wide, n_narrow = lax.axis_size("wide"), lax.axis_size("narrow")
-    everyone = ("wide", "narrow")
     total = leaves * n_wide * n_narrow
-    leaf_mass = masses.reshape(leaves, members)
     f32 = jnp.float32
 
-    patch = pl.pallas_call(
-        patch_kernel,
-        out_shape=jax.ShapeDtypeStruct((leaves, PATCH), f32),
+    packed, book = pl.pallas_call(
+        pack_kernel,
+        out_shape=(
+            jax.ShapeDtypeStruct((leaves, 2 * PATCH), f32),
+            jax.ShapeDtypeStruct((leaves, 8, members), f32),
+        ),
+        in_specs=[SMEM, SMEM, VMEM, VMEM],
+        out_specs=(VMEM, VMEM),
+        name="pack",
+    )(leaf_cell, tile_lists, fraction, masses.reshape(1, -1))
+    copies = n_wide - 1 + n_narrow - 1
+    gathered, books = pl.pallas_call(
+        gather_kernel,
+        out_shape=(
+            jax.ShapeDtypeStruct((n_wide, n_narrow, leaves, 2 * PATCH), f32),
+            jax.ShapeDtypeStruct((5, leaves, 8, members), f32),
+        ),
         in_specs=[VMEM, VMEM],
+        out_specs=(VMEM, VMEM),
+        scratch_shapes=[
+            pltpu.SemaphoreType.DMA((2,)),
+            pltpu.SemaphoreType.DMA((copies + 4,)),
+            pltpu.SemaphoreType.DMA((copies + 4,)),
+        ],
+        compiler_params=pltpu.CompilerParams(collective_id=0, has_side_effects=True),
+        name="gather",
+    )(packed, book)
+    gathered = gathered.reshape(total, 2 * PATCH)
+    notes = books[:, :, 4, 0:5].astype(jnp.int32)
+    short = pl.pallas_call(
+        functools.partial(pair_kernel, leaves, slots),
+        out_shape=jax.ShapeDtypeStruct((leaves, 8, members), f32),
+        in_specs=[SMEM, SMEM, VMEM],
         out_specs=VMEM,
-        name="patch",
-    )(fraction, leaf_mass)
-    cell_f = leaf_cell.astype(f32)
-    packed = jnp.concatenate([patch, cell_f.T], axis=1)
-    gathered = lax.all_gather(packed, everyone, axis=0, tiled=True)
-    cells = gathered[:, PATCH : PATCH + 3].T
-
-    extents = jnp.asarray([PX - 1.0, PY - 1.0, PZ - 1.0], dtype=f32)
-    place = fraction.reshape(3, leaves, members) * extents[:, None, None] + 0.5
-    place = jnp.transpose(cell_f[:, :, None] + place, (1, 0, 2))
-    notes = jnp.concatenate([tile_lists.T.astype(f32), cell_f.T], axis=1)
-    notes = jnp.pad(notes, ((0, 0), (0, members - notes.shape[1])))
-    book = jnp.concatenate([place, leaf_mass[:, None], notes[:, None]], axis=1)
-    books = [book]
-    for axis, by in (("wide", -1), ("wide", 1), ("narrow", -1), ("narrow", 1)):
-        peers = lax.axis_size(axis)
-        books.append(lax.ppermute(book, axis, [(i, (i + by) % peers) for i in range(peers)]))
-    books = jnp.stack(books)
-    lists = books[:, :, 4, 0:2].astype(jnp.int32)
-    corner = books[:, :, 4, 2:5]
-    chosen = jnp.minimum(exports, leaves - 1).reshape(-1)
-    target_at = jnp.concatenate([jnp.arange(leaves, dtype=jnp.int32), chosen])
-    rank_at = jnp.concatenate(
-        [jnp.zeros((leaves,), jnp.int32), jnp.repeat(jnp.arange(1, 5, dtype=jnp.int32), slots)]
-    )
-    live = jnp.concatenate([jnp.ones((leaves,), f32), (exports < leaves).astype(f32).reshape(-1)])
-    source_at = rank_at[None, :] * leaves + lists[rank_at, target_at].T
-    apart = corner.reshape(5 * leaves, 3)[source_at] - cell_f.T[target_at][None]
-    shift = -float(G) * jnp.floor(apart / G + 0.5)
-    shift = jnp.transpose(shift, (0, 2, 1)).reshape(6, -1)
-    jobs = target_at.shape[0]
-    sources = jnp.pad(books.reshape(5 * leaves, 5, members), ((0, 0), (0, 3), (0, 0)))
-    short = pl.pallas_call(
-        functools.partial(pair_kernel, leaves, jobs),
-        out_shape=jax.ShapeDtypeStruct((leaves, 8, members), f32),
-        in_specs=[SMEM, SMEM, SMEM, SMEM, VMEM],
-        out_specs=VMEM,
-        cost_estimate=pl.CostEstimate(
-            flops=jobs * 2 * members * members * 60, bytes_accessed=2**20, transcendentals=0
-        ),
         name="pairs",
-    )(source_at, target_at, shift, live, sources)
+    )(exports, notes, books)
 
     nz = -(-(G // 2 + 1) // n_narrow)
     ny = G // n_wide
@@ -351,8 +481,7 @@
         out_shape=jax.ShapeDtypeStruct((modes, 2 * G), f32),
         in_specs=[
             SMEM,
-            pl.BlockSpec((size, PATCH + 3), lambda i: (i, 0)),
-            pl.BlockSpec((3, size), lambda i: (0, i)),
+            pl.BlockSpec((size, 2 * PATCH), lambda i: (i, 0)),
         ],
         out_specs=pl.BlockSpec((modes, 2 * G), lambda i: (0, 0)),
         scratch_shapes=[
@@ -361,7 +490,7 @@
         ],
         compiler_params=params,
         name="forward",
-    )(origin, gathered, cells)
+    )(origin, gathered)
     partial = pl.pallas_call(
         functools.partial(inverse_kernel, ny, chunk),
         grid=(blocks,),
@@ -369,7 +498,7 @@
         in_specs=[
             SMEM,
             pl.BlockSpec((modes, 2 * G), lambda i: (0, 0)),
-            pl.BlockSpec((3, size), lambda i: (0, i)),
+            pl.BlockSpec((size, 2 * PATCH), lambda i: (i, 0)),
         ],
         out_specs=pl.BlockSpec((size, 3 * PATCH), lambda i: (i, 0)),
         scratch_shapes=[
@@ -379,8 +508,23 @@
         ],
         compiler_params=params,
         name="inverse",
-    )(origin, spectrum, cells)
-    field = lax.psum_scatter(partial, everyone, scatter_dimension=0, tiled=True)
+    )(origin, spectrum, gathered)
+    block = (leaves, 3 * PATCH)
+    field = pl.pallas_call(
+        scatter_kernel,
+        out_shape=jax.ShapeDtypeStruct(block, f32),
+        in_specs=[VMEM],
+        out_specs=VMEM,
+        scratch_shapes=[
+            pltpu.VMEM((n_wide - 1, n_narrow) + block, f32),
+            pltpu.VMEM((n_narrow,) + block, f32),
+            pltpu.VMEM((n_narrow - 1,) + block, f32),
+            pltpu.SemaphoreType.DMA((copies,)),
+            pltpu.SemaphoreType.DMA((copies,)),
+        ],
+        compiler_params=pltpu.CompilerParams(collective_id=1, has_side_effects=True),
+        name="scatter",
+    )(partial.reshape((n_wide, n_narrow) + block))
     return pl.pallas_call(
         sample_kernel,
         out_shape=jax.ShapeDtypeStruct((3, leaves * members), f32),

time: 255 us -> 72.2 us (0.28)
  waiting for transfers between devices: 111 us -> 0 us
  blocking collectives: 70.8 us -> 0 us
  Pallas kernels: 39.5 us -> 68.2 us
  between operations: 13.5 us -> 0.02 us
  starting transfers between devices: 6.97 us -> 0 us
  local copies, waits for them, and re-layouts: 7.66 us -> 2.27 us
  other arithmetic: 4.87 us -> 1.25 us
    unnamed x2 -> x0, waiting for transfers between devices: 111 us -> none
    all_gather x1 -> x0, blocking collectives: 70.8 us -> none  [local(): gathered = lax.all_gather(packed, everyone, axis=0, tiled=True)]
    pallas_call x2 -> x4, Pallas kernels: 10.2 us -> 38.5 us  [the longest x1 14.9 us: local(): pl.pallas_call(gather_kernel, out_shape=(jax.ShapeDtypeStruct((n_wide, n_...]
    ppermute x4 -> x0, starting transfers between devices: 6.97 us -> none  [local(): lax.ppermute(book, axis, [(i, (i + by) % peers) for i in range(peers)])]
    concatenate x5 -> x0, other arithmetic: 2.64 us -> none  [the longest x1 0.69 us: local(): book = jnp.concatenate([place, leaf_mass[:, None], notes[:, None]], axis=1)]
  transfers between devices with their start and end apart: 5 -> 0, of which waited for: 1 -> 0; matrix products, arithmetic and copies ran while one was open for 3% -> 0% of each run, Pallas kernels for 15% -> 0%
where the time goes in v2:
time: 72.2 us; the launch traced here: 71.7 us
  Pallas kernels  68.2 us (94%)
  local copies, waits for them, and re-layouts  2.27 us (3%)
  other arithmetic  1.25 us (2%)
    pallas_call x1, Pallas kernels, local(): pl.pallas_call(functools.partial(inverse_kernel, ny, chunk), grid=(blocks...  17 us
    pallas_call x1, Pallas kernels, local(): pl.pallas_call(gather_kernel, out_shape=(jax.ShapeDtypeStruct((n_wide, n_...  14.9 us
    pallas_call x1, Pallas kernels, local(): pl.pallas_call(scatter_kernel, out_shape=jax.ShapeDtypeStruct(block, f32)...  13.3 us
    pallas_call x1, Pallas kernels, local(): pl.pallas_call(functools.partial(forward_kernel, ny, chunk), grid=(blocks...  10.9 us
    pallas_call x1, Pallas kernels, local(): pl.pallas_call(functools.partial(pair_kernel, leaves, slots), out_shape=j...  8.37 us
    pallas_call x1, Pallas kernels, local(): pl.pallas_call(pack_kernel, out_shape=(jax.ShapeDtypeStruct((leaves, 2 *...  1.92 us
    pallas_call x1, Pallas kernels, local(): pl.pallas_call(sample_kernel, out_shape=jax.ShapeDtypeStruct((3, leaves *...  1.88 us

profile of v2, /device:TPU:0, one launch (start us, length us, event | category | flops | bytes accessed | tf_op | source)
XLA Modules:
  0.0 71.7 jit_solution(6526422303352628858)
XLA Ops:
  0.0 0.6 pad_add_fusion.origin
  0.6 1.3 %copy.7.exports = s32[4,2]{1,0:T(4,128)} copy(s32[4,2]{0,1:T(2,128)} %param.8) | data formatting | bytes 64 | tf_op args[3]
  2.0 1.9 %pack.1 = (f32[8,256]{1,0:T(8,128)}, f32[8,8,128]{2,1,0:T(8,128)}) custom-call(s32[3,8]{1,0:T(4,128)} %leaf_cell.1, s32[2,8]{1,0:T(2,128)} %tile_lists.1, f32[3,1024]{1,0:T(4,128)} %fraction.3, f32[1,1024]{1,0:T(1,128)} %bitcast.10), custom_call_target="tpu_custom_call" | custom-call | tf_op jit(solution)/shard_map/pack/pallas_call | solution.py:430
  3.9 14.9 %gather.1 = (f32[8,4,8,256]{3,2,1,0:T(8,128)}, f32[5,8,8,128]{3,2,1,0:T(8,128)}) custom-call(f32[8,256]{1,0:T(8,128)} %get-tuple-element.9.packed, f32[8,8,128]{2,1,0:T(8,128)} %get-tuple-element.10.book), custom_call_target="tpu_custom_call" | custom-call | tf_op jit(solution)/shard_map/gather/pallas_call | solution.py:441
  18.7 0.9 %copy.6 = f32[5,8,8,128]{3,1,0,2:T(8,128)S(1)} copy(f32[5,8,8,128]{3,2,1,0:T(8,128)} %get-tuple-element.12.books) | data formatting | bytes 327680 | tf_op jit(solution)/shard_map/gather/pallas_call | solution.py:441
  19.7 0.6 fusion.notes
  20.3 8.4 %pairs.1.short = f32[8,8,128]{2,1,0:T(8,128)} custom-call(s32[4,2]{1,0:T(4,128)} %copy.7.exports, s32[5,8,5]{2,1,0:T(8,128)} %fusion.notes, f32[5,8,8,128]{3,2,1,0:T(8,128)} %get-tuple-element.12.books), custom_call_target="tpu_custom_call" | custom-call | tf_op jit(solution)/shard_map/pairs/pallas_call | solution.py:459
  28.7 10.9 %forward.1.spectrum = f32[1056,512]{1,0:T(8,128)} custom-call(s32[2]{0:T(128)} %pad_add_fusion.origin, f32[256,256]{1,0:T(8,128)} %bitcast.8), custom_call_target="tpu_custom_call" | custom-call | tf_op jit(solution)/shard_map/forward/pallas_call | solution.py:478
  39.6 17.0 %inverse.1 = f32[256,384]{1,0:T(8,128)} custom-call(s32[2]{0:T(128)} %pad_add_fusion.origin, f32[1056,512]{1,0:T(8,128)} %forward.1.spectrum, f32[256,256]{1,0:T(8,128)} %bitcast.9), custom_call_target="tpu_custom_call" | custom-call | tf_op jit(solution)/shard_map/inverse/pallas_call | solution.py:494
  56.5 13.3 %scatter.1.field = f32[8,384]{1,0:T(8,128)} custom-call(f32[8,4,8,384]{3,2,1,0:T(8,128)} %bitcast.7), custom_call_target="tpu_custom_call" | custom-call | tf_op jit(solution)/shard_map/scatter/pallas_call | solution.py:513
  69.8 1.9 %sample.1 = f32[3,1024]{1,0:T(4,128)} custom-call(f32[8,384]{1,0:T(8,128)} %scatter.1.field, f32[3,1024]{1,0:T(4,128)} %fraction.3, f32[8,8,128]{2,1,0:T(8,128)} %pairs.1.short), custom_call_target="tpu_custom_call" | custom-call | tf_op jit(solution)/shard_map/sample/pallas_call | solution.py:528

commit v3 on v2

--- a/solution.py
+++ b/solution.py
@@ -225,142 +225,192 @@
         copy.wait_send()
 
 
-def mode_columns(base, rows, ny, origin):
-    w = base + iota((rows, 1), 0)
-    kz = origin[0] + w // ny
-    ky = origin[1] + w % ny
-    return ky, kz
-
-
-def forward_kernel(ny, chunk, origin, patches, out, e_hi, e_lo):
-    step = pl.program_id(0)
+def modes_at(index, ny, origin):
+    return origin[1] + index % ny, origin[0] + index // ny
+
+
+def x_basis(x, lane):
+    half = G // 2
+    wave = jnp.where(lane > half, lane - half, lane).astype(jnp.float32)
+    turn = jnp.where(lane > half, float(G // 4), 0.0)
+    return sincos(x * wave - turn)[0]
+
+
+def forward_tables(patches, e_hi, e_lo, p_cat):
     size = patches.shape[0]
-    modes = out.shape[0]
     x_col = patches[:, PATCH : PATCH + 1]
-    kx = iota((size, G), 1).astype(jnp.float32)
+    lane = iota((size, G), 1)
+    group = iota((size, 4 * PATCH_YZ), 1) // PATCH_YZ
     for a in range(PX):
-        c, s = sincos((x_col + float(a)) * kx)
-        r0, r1 = a * size, (PX + a) * size
-        for part, r, col in ((c, r0, 0), (-s, r0, G), (s, r1, 0), (c, r1, G)):
-            hi, lo = split(part)
-            e_hi[r : r + size, col : col + G] = hi
-            e_lo[r : r + size, col : col + G] = lo
-    cells = patches[:, PATCH:].T
-    y_row = cells[1:2, :]
-    z_row = cells[2:3, :]
-
-    def body(i, carry):
-        at = pl.ds(pl.multiple_of(i * chunk, 8), chunk)
-        ky, kz = mode_columns(i * chunk, chunk, ny, origin)
-        kyf, kzf = ky.astype(jnp.float32), kz.astype(jnp.float32)
-        lane = iota((1, PATCH_YZ), 1)
-        tc, ts = sincos(
-            kyf * (lane // PZ).astype(jnp.float32) + kzf * (lane % PZ).astype(jnp.float32)
-        )
-        tc, ts = split(tc), split(ts)
-        c, s = sincos(kyf * y_row + kzf * z_row)
-        real, imag = [], []
-        for a in range(PX):
-            p = split(patches[:, a * PATCH_YZ : (a + 1) * PATCH_YZ])
-            fc = dot3(tc, p, ((1,), (1,)))
-            fs = dot3(ts, p, ((1,), (1,)))
-            real.append(fc * c - fs * s)
-            imag.append(-(fc * s + fs * c))
-        m = split(jnp.concatenate(real + imag, axis=1))
-        got = dot3(m, (e_hi[...], e_lo[...]))
-
-        @pl.when(step == 0)
-        def _():
-            out[at, :] = got
-
-        @pl.when(step > 0)
-        def _():
-            out[at, :] += got
-
-        @pl.when(step == pl.num_programs(0) - 1)
-        def _():
-            unit = 2.0 * math.pi / G
-            fx = folded(iota((1, G), 1)) * unit
-            fy, fz = folded(ky) * unit, folded(kz) * unit
-            total = fx * fx + (fy * fy + fz * fz)
-            divisor = jnp.where(total > 0, total, 1.0)
-            green = jnp.where(
-                total > 0, -4.0 * math.pi * jnp.exp(-total * (SCREEN * SCREEN)) / divisor, 0.0
-            )
-            for col in (0, G):
-                out[at, col : col + G] = out[at, col : col + G] * green
-
-        return carry
-
-    lax.fori_loop(0, modes // chunk, body, 0)
-
-
-def inverse_kernel(ny, chunk, origin, spectrum, leaf_rows, out, e_hi, e_lo, acc):
-    size = leaf_rows.shape[0]
-    cells = leaf_rows[:, PATCH:].T
-    modes = spectrum.shape[0]
-    width = PX * size
-    kx = iota((G, size), 0).astype(jnp.float32)
+        at = slice(a * size, (a + 1) * size)
+        e_hi[at, :], e_lo[at, :] = split(x_basis(x_col + float(a), lane))
+        p = jnp.concatenate([patches[:, a * PATCH_YZ : (a + 1) * PATCH_YZ]] * 4, axis=1)
+        hi = p.astype(jnp.bfloat16).astype(jnp.float32)
+        p_cat[at, :] = jnp.where(
+            group == 3, 0.0, jnp.where(group == 1, p - hi, hi)
+        ).astype(jnp.bfloat16)
+
+
+def inverse_tables(cells, e_hi, e_lo):
+    size = cells.shape[1]
+    row = iota((G, size), 0)
     for a in range(PX):
-        c, s = sincos((cells[0:1, :] + float(a)) * kx)
-        c0, c1 = a * size, (PX + a) * size
-        for part, r, col in ((c, 0, c0), (s, 0, c1), (-s, G, c0), (c, G, c1)):
-            hi, lo = split(part)
-            e_hi[r : r + G, col : col + size] = hi
-            e_lo[r : r + G, col : col + size] = lo
-    y_row = cells[1:2, :]
-    z_row = cells[2:3, :]
-    acc[...] = jnp.zeros_like(acc)
-
-    def body(i, carry):
-        at = pl.ds(pl.multiple_of(i * chunk, 8), chunk)
-        ky, kz = mode_columns(i * chunk, chunk, ny, origin)
-        c, s = sincos(ky.astype(jnp.float32) * y_row + kz.astype(jnp.float32) * z_row)
-        spec = spectrum[at, :]
-        e = (e_hi[...], e_lo[...])
-        lane_w = i * chunk + iota((1, chunk), 1)
-        kz_row = origin[0] + lane_w // ny
-        ky_row = origin[1] + lane_w % ny
-        row = iota((PATCH_YZ, 1), 0)
-        tc, ts = sincos(
-            ky_row.astype(jnp.float32) * (row // PZ).astype(jnp.float32)
-            + kz_row.astype(jnp.float32) * (row % PZ).astype(jnp.float32)
-        )
-        half = G // 2
-        weight = jnp.where(
-            (kz_row == 0) | (kz_row == half), 1.0, jnp.where(kz_row < half, 2.0, 0.0)
-        ) * (1.0 / float(G * G * G))
-        tc, ts = tc * weight, ts * weight
-        dy, dz = slope(ky_row), slope(kz_row)
-
-        def fields(source, cos_rows, sin_rows):
-            p = dot3(split(source), e)
-            total = None
-            real, imag = [], []
-            for a in range(PX):
-                pr = p[:, a * size : (a + 1) * size]
-                pi = p[:, (PX + a) * size : (PX + a + 1) * size]
-                real.append(pr * c - pi * s)
-                imag.append(pr * s + pi * c)
-            real = split(jnp.concatenate(real, axis=1))
-            imag = split(jnp.concatenate(imag, axis=1))
-            return dot3(split(sin_rows), real) + dot3(split(cos_rows), imag)
-
-        dx = slope(iota((1, 2 * G), 1) % G)
-        acc[0:PATCH_YZ, :] += fields(spec * dx, tc, ts)
-        acc[PATCH_YZ:, :] += fields(
-            spec,
-            jnp.concatenate([tc * dy, tc * dz], axis=0),
-            jnp.concatenate([ts * dy, ts * dz], axis=0),
-        )
-        return carry
-
-    lax.fori_loop(0, modes // chunk, body, 0)
+        at = slice(a * size, (a + 1) * size)
+        e_hi[:, at], e_lo[:, at] = split(x_basis(cells[0:1, :] + float(a), row))
+
+
+def phases(base, chunk, ny, origin, cells):
+    ky, kz = modes_at(base + iota((chunk, 1), 0), ny, origin)
+    return sincos(ky.astype(jnp.float32) * cells[1:2, :] + kz.astype(jnp.float32) * cells[2:3, :])
+
+
+def forward_chunk(base, chunk, ny, origin, phase, e, p_cat):
+    ky, kz = modes_at(base + iota((chunk, 1), 0), ny, origin)
+    lane = iota((1, 4 * PATCH_YZ), 1)
+    cell = lane % PATCH_YZ
+    group = lane // PATCH_YZ
+    tables = jnp.concatenate(
+        sincos(
+            ky.astype(jnp.float32) * (cell // PZ).astype(jnp.float32)
+            + kz.astype(jnp.float32) * (cell % PZ).astype(jnp.float32)
+        ),
+        axis=0,
+    )
+    hi = tables.astype(jnp.bfloat16).astype(jnp.float32)
+    tables = jnp.where(group == 3, 0.0, jnp.where(group == 2, tables - hi, hi))
+    f = lax.dot_general(
+        tables.astype(jnp.bfloat16),
+        p_cat,
+        (((1,), (1,)), ((), ())),
+        preferred_element_type=jnp.float32,
+    )
+    fc, fs = f[:chunk], f[chunk:]
+    c, s = (jnp.concatenate([part] * PX, axis=1) for part in phase)
+    m = jnp.concatenate([fc * c - fs * s, -(fc * s + fs * c)], axis=0)
+    return dot3(split(m), e)
+
+
+def apply_green(base, chunk, ny, origin, q):
+    ky, kz = modes_at(base + iota((chunk, 1), 0), ny, origin)
+    half = G // 2
+    lane = iota((1, G), 1)
+    unit = 2.0 * math.pi / G
+    fx = jnp.where(lane > half, lane - half, lane).astype(jnp.float32) * unit
+    fy, fz = folded(ky) * unit, folded(kz) * unit
+    total = fx * fx + (fy * fy + fz * fz)
+    divisor = jnp.where(total > 0, total, 1.0)
+    green = jnp.where(
+        total > 0, -4.0 * math.pi * jnp.exp(-total * (SCREEN * SCREEN)) / divisor, 0.0
+    )
+    green = green * jnp.where(lane % half == 0, 1.0, 2.0)
+    return q * jnp.concatenate([green, green], axis=0)
+
+
+def inverse_chunk(base, chunk, ny, origin, phase, e, h, acc):
+    half = G // 2
+    dx = slope(iota((1, half), 1))
+    hx = jnp.concatenate([-(h[:, half:] * dx), h[:, :half] * dx], axis=1)
+    lane = iota((1, 2 * chunk), 1)
+    ky, kz = modes_at(base + lane % chunk, ny, origin)
+    row = iota((PATCH_YZ, 1), 0)
+    turn = jnp.where(lane < chunk, float(G // 4), 0.0)
+    weight = jnp.where(
+        (kz == 0) | (kz == half), 1.0, jnp.where(kz < half, 2.0, 0.0)
+    ) * (1.0 / float(G * G * G))
+    angle = ky.astype(jnp.float32) * (row // PZ).astype(jnp.float32) + kz.astype(jnp.float32) * (
+        row % PZ
+    ).astype(jnp.float32)
+    slopes = sincos(angle - turn)[0] * weight
+    c, s = (jnp.concatenate([part] * PX, axis=1) for part in phase)
+
+    def add(source, at, table):
+        p = dot3(split(source), e)
+        real, imag = p[:chunk], p[chunk:]
+        turned = split(jnp.concatenate([real * c - imag * s, real * s + imag * c], axis=0))
+        hi, lo = split(table)
+        rows = table.shape[0]
+        dot = functools.partial(jnp.dot, preferred_element_type=jnp.float32)
+        both = dot(jnp.concatenate([hi, lo], axis=0), turned[0])
+        acc[at, :] += both[:rows] + (both[rows:] + dot(hi, turned[1]))
+
+    cosine = sincos(angle - turn + float(G // 4))[0] * weight
+    add(hx, slice(0, PATCH_YZ), cosine)
+    add(
+        h,
+        slice(PATCH_YZ, 3 * PATCH_YZ),
+        jnp.concatenate([slopes * slope(ky), slopes * slope(kz)], axis=0),
+    )
+
+
+def write_field(acc, out):
+    size = out.shape[0]
     for f in range(3):
         for a in range(PX):
             block = acc[f * PATCH_YZ : (f + 1) * PATCH_YZ, a * size : (a + 1) * size]
             col = f * PATCH + a * PATCH_YZ
             out[:, col : col + PATCH_YZ] = block.T
+
+
+def whole_kernel(ny, chunk, modes, origin, patches, out, e_hi, e_lo, p_cat, i_hi, i_lo, acc):
+    cells = patches[:, PATCH:].T
+    forward_tables(patches, e_hi, e_lo, p_cat)
+    inverse_tables(cells, i_hi, i_lo)
+    acc[...] = jnp.zeros_like(acc)
+
+    def body(i, carry):
+        base = i * chunk
+        phase = phases(base, chunk, ny, origin, cells)
+        q = forward_chunk(base, chunk, ny, origin, phase, (e_hi[...], e_lo[...]), p_cat[...])
+        h = apply_green(base, chunk, ny, origin, q)
+        inverse_chunk(base, chunk, ny, origin, phase, (i_hi[...], i_lo[...]), h, acc)
+        return carry
+
+    lax.fori_loop(0, modes // chunk, body, 0)
+    write_field(acc, out)
+
+
+def forward_kernel(ny, chunk, origin, patches, out, e_hi, e_lo, p_cat):
+    step = pl.program_id(0)
+    cells = patches[:, PATCH:].T
+    forward_tables(patches, e_hi, e_lo, p_cat)
+
+    @pl.when(step == 0)
+    def _():
+        out[...] = jnp.zeros_like(out)
+
+    def body(i, carry):
+        base = i * chunk
+        at = pl.ds(pl.multiple_of(2 * base, 8), 2 * chunk)
+        phase = phases(base, chunk, ny, origin, cells)
+        out[at, :] += forward_chunk(
+            base, chunk, ny, origin, phase, (e_hi[...], e_lo[...]), p_cat[...]
+        )
+
+        @pl.when(step == pl.num_programs(0) - 1)
+        def _():
+            out[at, :] = apply_green(base, chunk, ny, origin, out[at, :])
+
+        return carry
+
+    lax.fori_loop(0, out.shape[0] // (2 * chunk), body, 0)
+
+
+def inverse_kernel(ny, chunk, origin, spectrum, patches, out, i_hi, i_lo, acc):
+    cells = patches[:, PATCH:].T
+    inverse_tables(cells, i_hi, i_lo)
+    acc[...] = jnp.zeros_like(acc)
+
+    def body(i, carry):
+        base = i * chunk
+        at = pl.ds(pl.multiple_of(2 * base, 8), 2 * chunk)
+        phase = phases(base, chunk, ny, origin, cells)
+        inverse_chunk(
+            base, chunk, ny, origin, phase, (i_hi[...], i_lo[...]), spectrum[at, :], acc
+        )
+        return carry
+
+    lax.fori_loop(0, spectrum.shape[0] // (2 * chunk), body, 0)
+    write_field(acc, out)
 
 
 def pair_kernel(leaves, slots, exports, notes, books, out):
@@ -475,40 +525,50 @@
     size = min(total, 256)
     blocks = total // size
     params = pltpu.CompilerParams(vmem_limit_bytes=56 * 2**20)
-    spectrum = pl.pallas_call(
-        functools.partial(forward_kernel, ny, chunk),
-        grid=(blocks,),
-        out_shape=jax.ShapeDtypeStruct((modes, 2 * G), f32),
-        in_specs=[
-            SMEM,
-            pl.BlockSpec((size, 2 * PATCH), lambda i: (i, 0)),
-        ],
-        out_specs=pl.BlockSpec((modes, 2 * G), lambda i: (0, 0)),
-        scratch_shapes=[
-            pltpu.VMEM((2 * PX * size, 2 * G), jnp.bfloat16),
-            pltpu.VMEM((2 * PX * size, 2 * G), jnp.bfloat16),
-        ],
-        compiler_params=params,
-        name="forward",
-    )(origin, gathered)
-    partial = pl.pallas_call(
-        functools.partial(inverse_kernel, ny, chunk),
-        grid=(blocks,),
-        out_shape=jax.ShapeDtypeStruct((total, 3 * PATCH), f32),
-        in_specs=[
-            SMEM,
-            pl.BlockSpec((modes, 2 * G), lambda i: (0, 0)),
-            pl.BlockSpec((size, 2 * PATCH), lambda i: (i, 0)),
-        ],
-        out_specs=pl.BlockSpec((size, 3 * PATCH), lambda i: (i, 0)),
-        scratch_shapes=[
-            pltpu.VMEM((2 * G, 2 * PX * size), jnp.bfloat16),
-            pltpu.VMEM((2 * G, 2 * PX * size), jnp.bfloat16),
-            pltpu.VMEM((3 * PATCH_YZ, PX * size), f32),
-        ],
-        compiler_params=params,
-        name="inverse",
-    )(origin, spectrum, gathered)
+    forward_scratch = [
+        pltpu.VMEM((PX * size, G), jnp.bfloat16),
+        pltpu.VMEM((PX * size, G), jnp.bfloat16),
+        pltpu.VMEM((PX * size, 4 * PATCH_YZ), jnp.bfloat16),
+    ]
+    inverse_scratch = [
+        pltpu.VMEM((G, PX * size), jnp.bfloat16),
+        pltpu.VMEM((G, PX * size), jnp.bfloat16),
+        pltpu.VMEM((3 * PATCH_YZ, PX * size), f32),
+    ]
+    field_shape = jax.ShapeDtypeStruct((total, 3 * PATCH), f32)
+    leaf_rows = pl.BlockSpec((size, 2 * PATCH), lambda i: (i, 0))
+    spectrum_all = pl.BlockSpec((2 * modes, G), lambda i: (0, 0))
+    if blocks == 1:
+        partial = pl.pallas_call(
+            functools.partial(whole_kernel, ny, chunk, modes),
+            out_shape=field_shape,
+            in_specs=[SMEM, VMEM],
+            out_specs=VMEM,
+            scratch_shapes=forward_scratch + inverse_scratch,
+            compiler_params=params,
+            name="transform",
+        )(origin, gathered)
+    else:
+        spectrum = pl.pallas_call(
+            functools.partial(forward_kernel, ny, chunk),
+            grid=(blocks,),
+            out_shape=jax.ShapeDtypeStruct((2 * modes, G), f32),
+            in_specs=[SMEM, leaf_rows],
+            out_specs=spectrum_all,
+            scratch_shapes=forward_scratch,
+            compiler_params=params,
+            name="forward",
+        )(origin, gathered)
+        partial = pl.pallas_call(
+            functools.partial(inverse_kernel, ny, chunk),
+            grid=(blocks,),
+            out_shape=field_shape,
+            in_specs=[SMEM, spectrum_all, leaf_rows],
+            out_specs=pl.BlockSpec((size, 3 * PATCH), lambda i: (i, 0)),
+            scratch_shapes=inverse_scratch,
+            compiler_params=params,
+            name="inverse",
+        )(origin, spectrum, gathered)
     block = (leaves, 3 * PATCH)
     field = pl.pallas_call(
         scatter_kernel,

time: 72.2 us -> 64.6 us (0.89)
  Pallas kernels: 68.2 us -> 61.2 us
    pallas_call x2 -> x1, Pallas kernels: 27.8 us -> 20.9 us  [local(): pl.pallas_call(functools.partial(whole_kernel, ny, chunk, modes), out_sha...]
where the time goes in v3:
time: 64.6 us; the launch traced here: 64.1 us
  Pallas kernels  61.2 us (95%)
  local copies, waits for them, and re-layouts  1.69 us (3%)
  other arithmetic  1.19 us (2%)
    pallas_call x1, Pallas kernels, local(): pl.pallas_call(functools.partial(whole_kernel, ny, chunk, modes), out_sha...  20.9 us
    pallas_call x1, Pallas kernels, local(): pl.pallas_call(gather_kernel, out_shape=(jax.ShapeDtypeStruct((n_wide, n_...  14.9 us
    pallas_call x1, Pallas kernels, local(): pl.pallas_call(scatter_kernel, out_shape=jax.ShapeDtypeStruct(block, f32)...  13.3 us
    pallas_call x1, Pallas kernels, local(): pl.pallas_call(functools.partial(pair_kernel, leaves, slots), out_shape=j...  8.37 us
    pallas_call x1, Pallas kernels, local(): pl.pallas_call(pack_kernel, out_shape=(jax.ShapeDtypeStruct((leaves, 2 *...  1.92 us
    pallas_call x1, Pallas kernels, local(): pl.pallas_call(sample_kernel, out_shape=jax.ShapeDtypeStruct((3, leaves *...  1.88 us

profile of v3, /device:TPU:0, one launch (start us, length us, event | category | flops | bytes accessed | tf_op | source)
XLA Modules:
  0.0 64.1 jit_solution(57570714113109615)
XLA Ops:
  0.0 1.9 %pack.1 = (f32[8,256]{1,0:T(8,128)}, f32[8,8,128]{2,1,0:T(8,128)}) custom-call(s32[3,8]{1,0:T(4,128)} %leaf_cell.1, s32[2,8]{1,0:T(2,128)} %tile_lists.1, f32[3,1024]{1,0:T(4,128)} %fraction.3, f32[1,1024]{1,0:T(1,128)} %bitcast.9), custom_call_target="tpu_custom_call" | custom-call | tf_op jit(solution)/shard_map/pack/pallas_call | solution.py:480
  1.9 14.9 %gather.1 = (f32[8,4,8,256]{3,2,1,0:T(8,128)}, f32[5,8,8,128]{3,2,1,0:T(8,128)}) custom-call(f32[8,256]{1,0:T(8,128)} %get-tuple-element.9.packed, f32[8,8,128]{2,1,0:T(8,128)} %get-tuple-element.10.book), custom_call_target="tpu_custom_call" | custom-call | tf_op jit(solution)/shard_map/gather/pallas_call | solution.py:491
  16.8 0.9 %copy.6 = f32[5,8,8,128]{3,1,0,2:T(8,128)S(1)} copy(f32[5,8,8,128]{3,2,1,0:T(8,128)} %get-tuple-element.12.books) | data formatting | bytes 327680 | tf_op jit(solution)/shard_map/gather/pallas_call | solution.py:491
  17.7 0.0 copy-start
  17.7 0.6 fusion.notes
  18.3 0.1 copy-done
  18.4 0.7 %copy.7.exports = s32[4,2]{1,0:T(4,128)} copy(s32[4,2]{0,1:T(2,128)S(1)} %copy-done) | data formatting | bytes 64 | tf_op args[3]
  19.1 8.4 %pairs.1.short = f32[8,8,128]{2,1,0:T(8,128)} custom-call(s32[4,2]{1,0:T(4,128)} %copy.7.exports, s32[5,8,5]{2,1,0:T(8,128)} %fusion.notes, f32[5,8,8,128]{3,2,1,0:T(8,128)} %get-tuple-element.12.books), custom_call_target="tpu_custom_call" | custom-call | tf_op jit(solution)/shard_map/pairs/pallas_call | solution.py:509
  27.4 0.6 pad_add_fusion.origin
  28.0 20.9 %transform.1 = f32[256,384]{1,0:T(8,128)} custom-call(s32[2]{0:T(128)} %pad_add_fusion.origin, f32[256,256]{1,0:T(8,128)} %bitcast.8), custom_call_target="tpu_custom_call" | custom-call | tf_op jit(solution)/shard_map/transform/pallas_call | solution.py:542
  48.9 13.3 %scatter.1.field = f32[8,384]{1,0:T(8,128)} custom-call(f32[8,4,8,384]{3,2,1,0:T(8,128)} %bitcast.7), custom_call_target="tpu_custom_call" | custom-call | tf_op jit(solution)/shard_map/scatter/pallas_call | solution.py:573
  62.2 1.9 %sample.1 = f32[3,1024]{1,0:T(4,128)} custom-call(f32[8,384]{1,0:T(8,128)} %scatter.1.field, f32[3,1024]{1,0:T(4,128)} %fraction.3, f32[8,8,128]{2,1,0:T(8,128)} %pairs.1.short), custom_call_target="tpu_custom_call" | custom-call | tf_op jit(solution)/shard_map/sample/pallas_call | solution.py:588
Async XLA Ops:
  17.7 0.7 %copy-start = (s32[4,2]{0,1:T(2,128)S(1)}, s32[4,2]{0,1:T(2,128)}, u32[]{:S(2)}) copy-start(s32[4,2]{0,1:T(2,128)} %param.8) | copy-start | bytes 100

commit v4 on v3

--- a/solution.py
+++ b/solution.py
@@ -188,43 +188,6 @@
         copy.wait_send()
 
 
-def scatter_kernel(partial, out, landed, mine, near, sends, recvs):
-    wide, narrow = peers_of("wide"), peers_of("narrow")
-    w, v = lax.axis_index("wide"), lax.axis_index("narrow")
-    greet(wide + narrow)
-    at = 0
-    first = []
-    for axis, s, ahead, _ in wide:
-        first.append(
-            remote(partial.at[ahead], landed.at[s - 1], sends.at[at], recvs.at[at], axis, ahead)
-        )
-        at += 1
-    for copy in first:
-        copy.start()
-    for copy in first:
-        copy.wait_recv()
-    total = partial[w]
-    for s in range(len(wide)):
-        total = total + landed[s]
-    mine[...] = total
-    second = []
-    for axis, s, ahead, _ in narrow:
-        second.append(
-            remote(mine.at[ahead], near.at[s - 1], sends.at[at], recvs.at[at], axis, ahead)
-        )
-        at += 1
-    for copy in second:
-        copy.start()
-    for copy in second:
-        copy.wait_recv()
-    total = mine[v]
-    for s in range(len(narrow)):
-        total = total + near[s]
-    out[...] = total
-    for copy in first + second:
-        copy.wait_send()
-
-
 def modes_at(index, ny, origin):
     return origin[1] + index % ny, origin[0] + index // ny
 
@@ -413,10 +376,8 @@
     write_field(acc, out)
 
 
-def pair_kernel(leaves, slots, exports, notes, books, out):
-    out[...] = jnp.zeros_like(out)
-
-    def job(rank, target, pick):
+def pair_jobs(leaves, slots, exports, notes, books, forces):
+    def job(j, rank, target):
         tgt = books[0, target]
         total = [0.0, 0.0, 0.0]
         for k in range(2):
@@ -441,32 +402,75 @@
             w = cols[:, 3:4] * screened * (inv * inv * inv)
             for c in range(3):
                 total[c] = total[c] + jnp.sum(w * d[c], axis=0, keepdims=True)
-        out[target, 0:3, :] += jnp.concatenate(total, axis=0) * pick
+        forces[j] = jnp.concatenate(total + [jnp.zeros((5,) + total[0].shape[1:], jnp.float32)], axis=0)
 
     def own(n, carry):
-        job(0, n, 1.0)
+        job(n, 0, n)
         return carry
 
     def guest(j, carry):
         face = j // slots
-        leaf = exports[face, j % slots]
-        job(face + 1, jnp.minimum(leaf, leaves - 1), (leaf < leaves).astype(jnp.float32))
+        job(leaves + j, face + 1, jnp.minimum(exports[face, j % slots], leaves - 1))
         return carry
 
     lax.fori_loop(0, leaves, own, 0)
     lax.fori_loop(0, 4 * slots, guest, 0)
 
 
-def sample_kernel(field, fraction, short, out):
-    leaves = field.shape[0]
+def finish_kernel(
+    exports, notes, books, fraction, partial, out, landed, mine, near, forces, w_hi, w_lo, sends, recvs
+):
+    wide, narrow = peers_of("wide"), peers_of("narrow")
+    w, v = lax.axis_index("wide"), lax.axis_index("narrow")
+    leaves = mine.shape[1]
+    slots = exports.shape[1]
     members = fraction.shape[1] // leaves
+    greet(wide + narrow)
+    at = 0
+    first = []
+    for axis, s, ahead, _ in wide:
+        first.append(
+            remote(partial.at[ahead], landed.at[s - 1], sends.at[at], recvs.at[at], axis, ahead)
+        )
+        at += 1
+    for copy in first:
+        copy.start()
+    pair_jobs(leaves, slots, exports, notes, books, forces)
+    for copy in first:
+        copy.wait_recv()
+    total = partial[w]
+    for s in range(len(wide)):
+        total = total + landed[s]
+    mine[...] = total
+    second = []
+    for axis, s, ahead, _ in narrow:
+        second.append(
+            remote(mine.at[ahead], near.at[s - 1], sends.at[at], recvs.at[at], axis, ahead)
+        )
+        at += 1
+    for copy in second:
+        copy.start()
+    short = []
     for n in range(leaves):
-        at = slice(n * members, (n + 1) * members)
-        w = split(leaf_weights(fraction[:, at]))
+        w_hi[n], w_lo[n] = split(leaf_weights(fraction[:, n * members : (n + 1) * members]))
+        force = forces[n]
+        for j in range(4 * slots):
+            mine_too = jnp.where(exports[j // slots, j % slots] == n, 1.0, 0.0)
+            force = force + forces[leaves + j] * mine_too
+        short.append(force)
+    for copy in second:
+        copy.wait_recv()
+    field = mine[v]
+    for s in range(len(narrow)):
+        field = field + near[s]
+    for n in range(leaves):
         values = jnp.concatenate(
             [field[n : n + 1, f * PATCH : (f + 1) * PATCH] for f in range(3)], axis=0
         )
-        out[:, at] = dot3(split(values), w) + short[n, 0:3, :]
+        got = dot3(split(values), (w_hi[n], w_lo[n]))
+        out[:, n * members : (n + 1) * members] = got + short[n][0:3, :]
+    for copy in first + second:
+        copy.wait_send()
 
 
 def local(fraction, masses, leaf_cell, exports, tile_lists):
@@ -506,14 +510,6 @@
     )(packed, book)
     gathered = gathered.reshape(total, 2 * PATCH)
     notes = books[:, :, 4, 0:5].astype(jnp.int32)
-    short = pl.pallas_call(
-        functools.partial(pair_kernel, leaves, slots),
-        out_shape=jax.ShapeDtypeStruct((leaves, 8, members), f32),
-        in_specs=[SMEM, SMEM, VMEM],
-        out_specs=VMEM,
-        name="pairs",
-    )(exports, notes, books)
-
     nz = -(-(G // 2 + 1) // n_narrow)
     ny = G // n_wide
     modes = nz * ny
@@ -570,28 +566,24 @@
             name="inverse",
         )(origin, spectrum, gathered)
     block = (leaves, 3 * PATCH)
-    field = pl.pallas_call(
-        scatter_kernel,
-        out_shape=jax.ShapeDtypeStruct(block, f32),
-        in_specs=[VMEM],
+    return pl.pallas_call(
+        finish_kernel,
+        out_shape=jax.ShapeDtypeStruct((3, leaves * members), f32),
+        in_specs=[SMEM, SMEM, VMEM, VMEM, VMEM],
         out_specs=VMEM,
         scratch_shapes=[
             pltpu.VMEM((n_wide - 1, n_narrow) + block, f32),
             pltpu.VMEM((n_narrow,) + block, f32),
             pltpu.VMEM((n_narrow - 1,) + block, f32),
+            pltpu.VMEM((leaves + 4 * slots, 8, members), f32),
+            pltpu.VMEM((leaves, PATCH, members), jnp.bfloat16),
+            pltpu.VMEM((leaves, PATCH, members), jnp.bfloat16),
             pltpu.SemaphoreType.DMA((copies,)),
             pltpu.SemaphoreType.DMA((copies,)),
         ],
         compiler_params=pltpu.CompilerParams(collective_id=1, has_side_effects=True),
-        name="scatter",
-    )(partial.reshape((n_wide, n_narrow) + block))
-    return pl.pallas_call(
-        sample_kernel,
-        out_shape=jax.ShapeDtypeStruct((3, leaves * members), f32),
-        in_specs=[VMEM, VMEM, VMEM],
-        out_specs=VMEM,
-        name="sample",
-    )(field, fraction, short)
+        name="finish",
+    )(exports, notes, books, fraction, partial.reshape((n_wide, n_narrow) + block))
 
 
 def solution(mesh):

time: 64.6 us -> 56 us (0.87)
  Pallas kernels: 61.2 us -> 52.3 us
    pallas_call x3 -> x1, Pallas kernels: 23.6 us -> 14.6 us  [local(): pl.pallas_call(finish_kernel, out_shape=jax.ShapeDtypeStruct((3, leaves *...]
    unnamed x3 -> x6, local copies, waits for them, and re-layouts: 0.74 us -> 2.06 us
    pallas_call x1, local copies, waits for them, and re-layouts: 0.95 us -> 0.03 us  [local(): pl.pallas_call(gather_kernel, out_shape=(jax.ShapeDtypeStruct((n_wide, n_...]
where the time goes in v4:
time: 56 us; the launch traced here: 55.6 us
  Pallas kernels  52.3 us (93%)
  local copies, waits for them, and re-layouts  2.09 us (4%)
  other arithmetic  1.18 us (2%)
    pallas_call x1, Pallas kernels, local(): pl.pallas_call(functools.partial(whole_kernel, ny, chunk, modes), out_sha...  20.9 us
    pallas_call x1, Pallas kernels, local(): pl.pallas_call(gather_kernel, out_shape=(jax.ShapeDtypeStruct((n_wide, n_...  14.8 us
    pallas_call x1, Pallas kernels, local(): pl.pallas_call(finish_kernel, out_shape=jax.ShapeDtypeStruct((3, leaves *...  14.6 us
    unnamed x6, local copies, waits for them, and re-layouts  2.06 us
    pallas_call x1, Pallas kernels, local(): pl.pallas_call(pack_kernel, out_shape=(jax.ShapeDtypeStruct((leaves, 2 *...  1.92 us

profile of v4, /device:TPU:0, one launch (start us, length us, event | category | flops | bytes accessed | tf_op | source)
XLA Modules:
  0.0 55.6 jit_solution(8435883782917087331)
XLA Ops:
  0.0 1.9 %pack.1 = (f32[8,256]{1,0:T(8,128)}, f32[8,8,128]{2,1,0:T(8,128)}) custom-call(s32[3,8]{1,0:T(4,128)} %leaf_cell.1, s32[2,8]{1,0:T(2,128)} %tile_lists.1, f32[3,1024]{1,0:T(4,128)} %fraction.3, f32[1,1024]{1,0:T(1,128)} %bitcast.9), custom_call_target="tpu_custom_call" | custom-call | tf_op jit(solution)/shard_map/pack/pallas_call | solution.py:484
  1.9 14.8 %gather.1 = (f32[8,4,8,256]{3,2,1,0:T(8,128)}, f32[5,8,8,128]{3,2,1,0:T(8,128)}) custom-call(f32[8,256]{1,0:T(8,128)} %get-tuple-element.9.packed, f32[8,8,128]{2,1,0:T(8,128)} %get-tuple-element.10.book), custom_call_target="tpu_custom_call" | custom-call | tf_op jit(solution)/shard_map/gather/pallas_call | solution.py:495
  16.8 0.6 %pad_add_fusion.origin = s32[2]{0:T(128)} fusion(s32[1]{0:T(128)} %bitcast.3, s32[1]{0:T(128)} %bitcast.2), kind=kLoop, calls=%fused_computation.2 | loop fusion | flops 2 | bytes 16 | tf_op jit(solution)/shard_map/stack | solution.py:518
  17.4 0.0 copy-start
  17.4 20.9 %transform.1 = f32[256,384]{1,0:T(8,128)} custom-call(s32[2]{0:T(128)} %pad_add_fusion.origin, f32[256,256]{1,0:T(8,128)} %bitcast.8), custom_call_target="tpu_custom_call" | custom-call | tf_op jit(solution)/shard_map/transform/pallas_call | solution.py:538
  38.3 0.0 copy-done
  38.3 0.0 copy-start.1
  38.3 0.6 %fusion.notes = s32[5,8,5]{2,1,0:T(8,128)} fusion(f32[5,8,8,128]{3,1,0,2:T(8,128)S(1)} %copy.6), kind=kLoop, calls=%fused_computation.1 | loop fusion | flops 200 | bytes 1600 | tf_op jit(solution)/shard_map/convert_element_type | solution.py:512
  38.9 0.1 copy-done.1
  39.0 0.7 %copy.7.exports = s32[4,2]{1,0:T(4,128)} copy(s32[4,2]{0,1:T(2,128)S(1)} %copy-done.1) | data formatting | bytes 64 | tf_op args[3]
  39.7 14.6 %finish.1 = f32[3,1024]{1,0:T(4,128)} custom-call(s32[4,2]{1,0:T(4,128)} %copy.7.exports, s32[5,8,5]{2,1,0:T(8,128)} %fusion.notes, f32[5,8,8,128]{3,2,1,0:T(8,128)} %get-tuple-element.11.books, f32[3,1024]{1,0:T(4,128)} %fraction.3, f32[8,4,8,384]{3,2,1,0:T(8,128)} %bitcast.7), custom_call_target="tpu_custom_call" | custom-call | tf_op jit(solution)/shard_map/finish/pallas_call | solution.py:569
  54.3 1.3 %copy.9 = f32[3,1024]{1,0:T(4,128)} copy(f32[3,1024]{1,0:T(4,128)} %finish.1) | data formatting | bytes 24576
  (1 shorter events, 0.0 us)
Async XLA Ops:
  17.4 20.9 %copy-start = (f32[5,8,8,128]{3,2,1,0:T(8,128)S(1)}, f32[5,8,8,128]{3,2,1,0:T(8,128)}, u32[]{:S(2)}) copy-start(f32[5,8,8,128]{3,2,1,0:T(8,128)} %get-tuple-element.11.books) | copy-start | bytes 491524
  38.3 0.7 %copy-start.1 = (s32[4,2]{0,1:T(2,128)S(1)}, s32[4,2]{0,1:T(2,128)}, u32[]{:S(2)}) copy-start(s32[4,2]{0,1:T(2,128)} %param.8) | copy-start | bytes 100

commit v5 on v4

--- a/solution.py
+++ b/solution.py
@@ -87,7 +87,7 @@
     return product
 
 
-def pack_kernel(leaf_cell, tile_lists, fraction, masses, packed, book):
+def pack(leaf_cell, tile_lists, fraction, masses, packed, book):
     leaves = packed.shape[0]
     members = masses.shape[1] // leaves
     lane = iota((1, members), 1)
@@ -118,12 +118,14 @@
     return [(axis, s, lax.rem(me + s, count), lax.rem(me + count - s, count)) for s in range(1, count)]
 
 
-def greet(groups):
+def greet(groups, meanwhile=None):
     barrier = pltpu.get_barrier_semaphore()
     for axis, _, ahead, _ in groups:
         pl.semaphore_signal(
             barrier, inc=1, device_id={axis: ahead}, device_id_type=pl.DeviceIdType.MESH
         )
+    if meanwhile is not None:
+        meanwhile()
     pl.semaphore_wait(barrier, len(groups))
 
 
@@ -138,20 +140,28 @@
     )
 
 
-def gather_kernel(packed, book, out, books, own, sends, recvs):
+def gather_kernel(
+    leaf_cell, tile_lists, fraction, masses, out, books, packed, book, own, sends, recvs
+):
     wide, narrow = peers_of("wide"), peers_of("narrow")
     w, v = lax.axis_index("wide"), lax.axis_index("narrow")
     keep = [
         pltpu.make_async_copy(packed, out.at[w, v], own.at[0]),
         pltpu.make_async_copy(book, books.at[0], own.at[1]),
     ]
-    for copy in keep:
-        copy.start()
-    greet(wide + narrow)
+
+    def fill():
+        pack(leaf_cell, tile_lists, fraction, masses, packed, book)
+        for copy in keep:
+            copy.start()
+        for copy in keep:
+            copy.wait()
+
+    greet(wide + narrow, fill)
     at = 0
     first = []
     for axis, s, ahead, _ in narrow:
-        first.append(remote(packed, out.at[w, v], sends.at[at], recvs.at[at], axis, ahead))
+        first.append(remote(out.at[w, v], out.at[w, v], sends.at[at], recvs.at[at], axis, ahead))
         at += 1
     for copy in first:
         copy.start()
@@ -164,20 +174,20 @@
             ("narrow", narrow[0][2]),
         )
     ):
-        near.append(remote(book, books.at[slot + 1], sends.at[at], recvs.at[at], axis, to))
+        near.append(remote(books.at[0], books.at[slot + 1], sends.at[at], recvs.at[at], axis, to))
         at += 1
-    for copy in keep:
-        copy.wait()
+    for copy in near:
+        copy.start()
     for copy, (axis, s, _, behind) in zip(first, narrow):
         remote(
-            packed, out.at[w, behind], sends.at[s - 1], recvs.at[s - 1], axis, behind
+            out.at[w, v], out.at[w, behind], sends.at[s - 1], recvs.at[s - 1], axis, behind
         ).wait_recv()
     second = []
     base = at
     for axis, s, ahead, _ in wide:
         second.append(remote(out.at[w], out.at[w], sends.at[at], recvs.at[at], axis, ahead))
         at += 1
-    for copy in second + near:
+    for copy in second:
         copy.start()
     for axis, s, _, behind in wide:
         i = base + s - 1
@@ -481,16 +491,6 @@
     total = leaves * n_wide * n_narrow
     f32 = jnp.float32
 
-    packed, book = pl.pallas_call(
-        pack_kernel,
-        out_shape=(
-            jax.ShapeDtypeStruct((leaves, 2 * PATCH), f32),
-            jax.ShapeDtypeStruct((leaves, 8, members), f32),
-        ),
-        in_specs=[SMEM, SMEM, VMEM, VMEM],
-        out_specs=(VMEM, VMEM),
-        name="pack",
-    )(leaf_cell, tile_lists, fraction, masses.reshape(1, -1))
     copies = n_wide - 1 + n_narrow - 1
     gathered, books = pl.pallas_call(
         gather_kernel,
@@ -498,16 +498,18 @@
             jax.ShapeDtypeStruct((n_wide, n_narrow, leaves, 2 * PATCH), f32),
             jax.ShapeDtypeStruct((5, leaves, 8, members), f32),
         ),
-        in_specs=[VMEM, VMEM],
+        in_specs=[SMEM, SMEM, VMEM, VMEM],
         out_specs=(VMEM, VMEM),
         scratch_shapes=[
+            pltpu.VMEM((leaves, 2 * PATCH), f32),
+            pltpu.VMEM((leaves, 8, members), f32),
             pltpu.SemaphoreType.DMA((2,)),
             pltpu.SemaphoreType.DMA((copies + 4,)),
             pltpu.SemaphoreType.DMA((copies + 4,)),
         ],
         compiler_params=pltpu.CompilerParams(collective_id=0, has_side_effects=True),
         name="gather",
-    )(packed, book)
+    )(leaf_cell, tile_lists, fraction, masses.reshape(1, -1))
     gathered = gathered.reshape(total, 2 * PATCH)
     notes = books[:, :, 4, 0:5].astype(jnp.int32)
     nz = -(-(G // 2 + 1) // n_narrow)

time: 56 us -> 53.5 us (0.955)
  Pallas kernels: 52.3 us -> 49.9 us
    pallas_call x1 -> x0, Pallas kernels: 1.92 us -> none  [local(): pl.pallas_call(pack_kernel, out_shape=(jax.ShapeDtypeStruct((leaves, 2 *...]
    pallas_call x1, Pallas kernels: 14.8 us -> 14.2 us  [local(): pl.pallas_call(gather_kernel, out_shape=(jax.ShapeDtypeStruct((n_wide, n_...]
where the time goes in v5:
time: 53.5 us; the launch traced here: 53.2 us
  Pallas kernels  49.9 us (93%)
  local copies, waits for them, and re-layouts  2.1 us (4%)
  other arithmetic  1.24 us (2%)
    pallas_call x1, Pallas kernels, local(): pl.pallas_call(functools.partial(whole_kernel, ny, chunk, modes), out_sha...  20.9 us
    pallas_call x1, Pallas kernels, local(): pl.pallas_call(finish_kernel, out_shape=jax.ShapeDtypeStruct((3, leaves *...  14.7 us
    pallas_call x1, Pallas kernels, local(): pl.pallas_call(gather_kernel, out_shape=(jax.ShapeDtypeStruct((n_wide, n_...  14.2 us
    unnamed x6, local copies, waits for them, and re-layouts  2.07 us

profile of v5, /device:TPU:0, one launch (start us, length us, event | category | flops | bytes accessed | tf_op | source)
XLA Modules:
  0.0 53.2 jit_solution(8564026127259718695)
XLA Ops:
  0.0 0.6 %pad_add_fusion.origin = s32[2]{0:T(128)} fusion(s32[1]{0:T(128)} %bitcast.3, s32[1]{0:T(128)} %bitcast.2), kind=kLoop, calls=%fused_computation.2 | loop fusion | flops 2 | bytes 16 | tf_op jit(solution)/shard_map/stack | solution.py:520
  0.6 14.2 %gather.1 = (f32[8,4,8,256]{3,2,1,0:T(8,128)}, f32[5,8,8,128]{3,2,1,0:T(8,128)}) custom-call(s32[3,8]{1,0:T(4,128)} %leaf_cell.1, s32[2,8]{1,0:T(2,128)} %tile_lists.1, f32[3,1024]{1,0:T(4,128)} %fraction.3, f32[1,1024]{1,0:T(1,128)} %bitcast.9), custom_call_target="tpu_custom_call" | custom-call | tf_op jit(solution)/shard_map/gather/pallas_call | solution.py:495
  14.9 0.0 copy-start
  14.9 20.9 %transform.1 = f32[256,384]{1,0:T(8,128)} custom-call(s32[2]{0:T(128)} %pad_add_fusion.origin, f32[256,256]{1,0:T(8,128)} %bitcast.8), custom_call_target="tpu_custom_call" | custom-call | tf_op jit(solution)/shard_map/transform/pallas_call | solution.py:540
  35.8 0.0 copy-done
  35.9 0.0 copy-start.1
  35.9 0.6 %fusion.notes = s32[5,8,5]{2,1,0:T(8,128)} fusion(f32[5,8,8,128]{3,1,0,2:T(8,128)S(1)} %copy.6), kind=kLoop, calls=%fused_computation.1 | loop fusion | flops 200 | bytes 1600 | tf_op jit(solution)/shard_map/convert_element_type | solution.py:514
  36.5 0.1 copy-done.1
  36.5 0.7 %copy.7.exports = s32[4,2]{1,0:T(4,128)} copy(s32[4,2]{0,1:T(2,128)S(1)} %copy-done.1) | data formatting | bytes 64 | tf_op args[3]
  37.2 14.7 %finish.1 = f32[3,1024]{1,0:T(4,128)} custom-call(s32[4,2]{1,0:T(4,128)} %copy.7.exports, s32[5,8,5]{2,1,0:T(8,128)} %fusion.notes, f32[5,8,8,128]{3,2,1,0:T(8,128)} %get-tuple-element.7.books, f32[3,1024]{1,0:T(4,128)} %fraction.3, f32[8,4,8,384]{3,2,1,0:T(8,128)} %bitcast.7), custom_call_target="tpu_custom_call" | custom-call | tf_op jit(solution)/shard_map/finish/pallas_call | solution.py:571
  51.9 1.3 %copy.9 = f32[3,1024]{1,0:T(4,128)} copy(f32[3,1024]{1,0:T(4,128)} %finish.1) | data formatting | bytes 24576
  (1 shorter events, 0.0 us)
Async XLA Ops:
  14.9 20.9 %copy-start = (f32[5,8,8,128]{3,2,1,0:T(8,128)S(1)}, f32[5,8,8,128]{3,2,1,0:T(8,128)}, u32[]{:S(2)}) copy-start(f32[5,8,8,128]{3,2,1,0:T(8,128)} %get-tuple-element.7.books) | copy-start | bytes 491524
  35.9 0.7 %copy-start.1 = (s32[4,2]{0,1:T(2,128)S(1)}, s32[4,2]{0,1:T(2,128)}, u32[]{:S(2)}) copy-start(s32[4,2]{0,1:T(2,128)} %param.8) | copy-start | bytes 100
